TPU v7x, 256 devices: a whole 4x4x8 slice. The times are simulated.
256 devices in a mesh: dp: 32 (over x_lo, z, core), tensor: 8 (over y, x_hi).
Axes of the slice: x: 4 (x_hi: 2, x_lo: 2; x = x_hi * 2 + x_lo), y: 4, z: 8, core: 2. Of those that a mesh axis runs over, the one named last changes fastest.
Arguments:
- tokens: bfloat16 [6144, 2048], P(('dp', 'tensor')), may hold values from -6 to 6
- grad_hidden: bfloat16 [6144, 5504], P('dp', 'tensor'), may hold values from -0.078125 to 0.078125
- width_in: bfloat16 [2048, 1024], P(None, 'tensor'), may hold values from -0.125 to 0.125
- gate_small: bfloat16 [1024, 2752], P(None, 'tensor'), may hold values from -0.1875 to 0.1875
- up_small: bfloat16 [1024, 2752], P(None, 'tensor'), may hold values from -0.1875 to 0.1875
- width_hidden: bfloat16 [5504, 2752], P('tensor'), may hold values from -0.109375 to 0.109375
Outputs:
- grad_width_in: float32 [2048, 1024], P('dp', 'tensor')
- grad_gate_small: float32 [1024, 2752], P('dp', 'tensor')
- grad_up_small: float32 [1024, 2752], P('dp', 'tensor')
- grad_width_hidden: float32 [5504, 2752], P('tensor', 'dp')
All inputs are finite; a program needn't handle non-finite values.
Results may differ from a plain program's by a relative error of at most 0.0085.
Values may be sent and summed in bfloat16 or wider, within the bound.
No kernel may reach another device: no remote copies, remote signals or barrier semaphores. Data moves between devices by JAX's collectives and lax.ppermute only.
A program may use at most 64 MiB of HBM per device.

v0:
```python
import jax
import jax.numpy as jnp
from jax import lax
from jax.sharding import Mesh
from jax.sharding import PartitionSpec as P

F32 = jnp.float32
BF16 = jnp.bfloat16
CHIPS = ("xl", "y", "xh")


def dot(left, right, dims):
    return lax.dot_general(left, right, (dims, ((), ())), preferred_element_type=F32)


def shift(value, axis, size, step):
    return lax.ppermute(value, axis, [(i, (i + step) % size) for i in range(size)])


def batched(left, right, left_dim, right_dim):
    dims = (((left_dim,), (right_dim,)), ((0,), (0,)))
    return lax.dot_general(left, right, dims, preferred_element_type=F32)


def swap(value, axis):
    return shift(value, axis, 2, 1)


def pick(index, first, second):
    return jnp.where(index == 0, first, second)


def ordered(index, own, other, axis):
    return pick(
        index, jnp.concatenate([own, other], axis), jnp.concatenate([other, own], axis)
    )


def place(canvas, piece, *start):
    return lax.dynamic_update_slice(canvas, piece, start)


def gather_four(value, axis, index, canvas, put):
    canvas = put(canvas, value, index)
    for step in (1, 3, 2):
        canvas = put(canvas, shift(value, axis, 4, step), (index - step) & 3)
    return canvas


def exchange(pieces, axes):
    return lax.all_to_all(pieces, axes, 0, 0, tiled=True)


def gather(value, axes, size):
    return exchange(jnp.broadcast_to(value[None], (size,) + value.shape), axes)


def gather_ring(value, z):
    tail = (0,) * value.ndim
    canvas = place(jnp.zeros((8,) + value.shape, value.dtype), value[None], z, *tail)

    def pass_on(k, carry):
        up, down, canvas = carry
        up, down = shift(up, "z", 8, 1), shift(down, "z", 8, -1)
        canvas = place(canvas, up, (z - 1 - k) & 7, *tail)
        return up, down, place(canvas, down, (z + 1 + k) & 7, *tail)

    return lax.fori_loop(0, 4, pass_on, (value[None], value[None], canvas))[2]


def after(value, *others):
    return lax.optimization_barrier((value,) + others)[0]


def step(tokens, grad_hidden, width_in, gate_small, up_small, width_hidden):
    xl, z, c, y, xh = (lax.axis_index(a) for a in ("xl", "z", "c", "y", "xh"))
    own, d_in = tokens.shape
    rows = own * 8
    wide = width_in.shape[1]
    ds = wide * 8
    fs = gate_small.shape[1]
    ff = width_hidden.shape[0]
    quarter = ff // 4
    part = ds // 32
    slot = fs // 4

    pair = ordered(xh, tokens, swap(tokens, "xh"), 0)
    all_tokens = gather_four(
        pair,
        "y",
        y,
        jnp.zeros((rows, d_in), BF16),
        lambda canvas, piece, i: place(canvas, piece, i * (2 * own), 0),
    )

    row0 = z * wide + (xl * 2 + c) * part
    mine = jnp.concatenate(
        [lax.dynamic_slice_in_dim(m, row0, part, 0) for m in (gate_small, up_small)], 0
    )
    proj = gather(mine, ("y", "xh"), 8)
    proj = jnp.transpose(proj, (1, 0, 2)).reshape(2 * part, 8 * fs)
    wt = dot(width_hidden, proj, ((1,), (1,))).astype(BF16)
    wt = wt.reshape(2, 2, quarter, 2 * part)
    keep, send = pick(c, wt[:, 0], wt[:, 1]), pick(c, wt[:, 1], wt[:, 0])
    wt = ordered(c, keep[None], swap(send, "c")[None], 0)
    keep, send = pick(xl, wt[:, 0], wt[:, 1]), pick(xl, wt[:, 1], wt[:, 0])
    wt = ordered(xl, keep[None], swap(send, "xl")[None], 0)
    blocks = [
        jnp.concatenate([wt[i, j, :, g * part : (g + 1) * part] for i in (0, 1) for j in (0, 1)], 1)
        for g in (0, 1)
    ]
    wt = jnp.concatenate(blocks, 0)
    wt_blocks = gather_ring(wt, z)
    wt = jnp.transpose(wt_blocks, (1, 0, 2)).reshape(2 * quarter, ds)

    narrow = dot(all_tokens, width_in, ((1,), (0,))).astype(BF16)

    gh = after(grad_hidden, narrow)
    gh = jnp.stack([gh[:, i * quarter : (i + 1) * quarter] for i in range(4)])
    gh = gh.reshape(2, 2, rows, quarter)
    keep, send = pick(c, gh[:, 0], gh[:, 1]), pick(c, gh[:, 1], gh[:, 0])
    gh = jnp.stack([keep, swap(send, "c")])
    keep, send = pick(xl, gh[:, 0], gh[:, 1]), pick(xl, gh[:, 1], gh[:, 0])
    gh = ordered(xl, keep[:, None], swap(send, "xl")[:, None], 1)

    narrow_part = narrow
    narrow = gather(narrow, CHIPS, 16).reshape(2, 8, rows, wide)
    narrow = jnp.transpose(narrow, (0, 2, 1, 3)).reshape(2 * rows, ds)
    narrow = jnp.concatenate([narrow, swap(narrow, "c")], 0)

    block = lax.dynamic_slice_in_dim(pick(c, after(gate_small, narrow_part), up_small), z * wide, wide, 0)
    block = pick(xl, block[:, : fs // 2], block[:, fs // 2 :])
    block = jnp.transpose(block.reshape(wide, 2, slot), (1, 2, 0))
    order = ("xl", "z", "c", "y", "xh")
    perm = []
    for i in range(256):
        sxl, sz, sc, sy, sxh = i // 128, i // 16 % 8, i // 8 % 2, i // 2 % 4, i % 2
        dz = (sy % 2) * 4 + sxh * 2 + sxl
        perm.append((i, (((sy // 2) * 8 + dz) * 2 + sc) * 8 + sz))
    cols = gather(lax.ppermute(block, order, perm), CHIPS, 16).reshape(2, 8, 2, slot, wide)
    cols = jnp.transpose(cols, (0, 2, 3, 1, 4)).reshape(4, slot, ds)
    other = swap(cols, "c")
    cols_g, cols_u = pick(c, cols, other), pick(c, other, cols)

    gate_big = dot(narrow, wt[:quarter], ((1,), (1,)))
    up_big = dot(narrow, wt[quarter:], ((1,), (1,)))
    upstream = gh.reshape(4 * rows, quarter).astype(F32)
    sig = jax.nn.sigmoid(gate_big)
    d_gate = (upstream * up_big * sig * (1.0 + gate_big * (1.0 - sig))).astype(BF16)
    d_up = (upstream * gate_big * sig).astype(BF16)
    d_both = jnp.concatenate([d_gate, d_up], 1)

    m_part = dot(narrow, d_both, ((0,), (0,))).reshape(2, 8, 2 * part, 2 * quarter)

    def back_of(d):
        rows_of = jnp.broadcast_to(d[None], (8,) + d.shape)
        return batched(rows_of, wt_blocks, 2, 1)

    other = back_of(d_both[2 * rows :]).astype(BF16)
    back = back_of(d_both[: 2 * rows]) + swap(other, "c").astype(F32)
    back = jnp.transpose(back.reshape(8, 2, rows, wide), (1, 0, 2, 3)).astype(BF16)
    back = back.reshape(16, rows, wide)
    m_part = exchange(jnp.transpose(m_part, (1, 0, 2, 3)).astype(BF16), "z")
    m_own = jnp.sum(m_part.astype(F32), 0).astype(BF16)
    m_all = gather_ring(m_own, z)
    m_all = jnp.transpose(m_all, (1, 0, 2, 3)).reshape(ds, 2 * quarter)

    d_narrow = jnp.sum(exchange(back, CHIPS).astype(F32), 0).astype(BF16)
    term = dot(all_tokens, d_narrow, ((0,), (0,))).astype(BF16)
    term = exchange(term.reshape(32, d_in // 32, wide), ("xl", "z", "c"))
    grad_width_in = jnp.sum(term.astype(F32), 0)

    wh = lax.dynamic_slice_in_dim(width_hidden, (xl * 2 + c) * quarter, quarter, 0)
    m_rows = m_own.reshape(2, 2, part, 2 * quarter)

    def small_of(m):
        m = jnp.stack([m[..., :quarter], m[..., quarter:]], 1).reshape(4 * part, quarter)
        return jnp.transpose(dot(wh, m, ((0,), (1,))).reshape(8, fs, 4 * part), (0, 2, 1))

    other = small_of(pick(c, m_rows[:, 1], m_rows[:, 0])).astype(BF16)
    small = small_of(pick(c, m_rows[:, 0], m_rows[:, 1])) + swap(other, "c").astype(F32)
    small = jnp.transpose(small.reshape(8, 2, 2 * part, fs), (1, 0, 2, 3)).astype(BF16)
    small = exchange(small.reshape(16, 2 * part, fs), CHIPS)
    small = jnp.sum(small.astype(F32), 0)
    grad_gate_small, grad_up_small = small[:part], small[part:]

    def hidden_of(m, cols):
        return batched(jnp.broadcast_to(m[None], (4,) + m.shape), cols, 1, 2)

    hidden = hidden_of(m_all[:, :quarter], cols_g) + hidden_of(m_all[:, quarter:], cols_u)
    hidden = hidden.astype(BF16).reshape(2, 2, quarter, slot)
    keep, send = pick(c, hidden[:, 0], hidden[:, 1]), pick(c, hidden[:, 1], hidden[:, 0])
    hidden = ordered(c, keep[None], swap(send, "c")[None], 0)
    keep, send = pick(xl, hidden[:, 0], hidden[:, 1]), pick(xl, hidden[:, 1], hidden[:, 0])
    hidden = ordered(xl, keep[None], swap(send, "xl")[None], 0).astype(F32).reshape(ff, slot)
    return (grad_width_in, grad_gate_small, grad_up_small, hidden)


def solution(mesh):
    grid = Mesh(mesh.devices.reshape(2, 8, 2, 4, 2), ("xl", "z", "c", "y", "xh"))
    dp, tensor = ("xl", "z", "c"), ("y", "xh")
    return jax.shard_map(
        step,
        mesh=grid,
        in_specs=(
            P(dp + tensor, None),
            P(dp, tensor),
            P(None, tensor),
            P(None, tensor),
            P(None, tensor),
            P(tensor, None),
        ),
        out_specs=(P(dp, tensor), P(dp, tensor), P(dp, tensor), P(tensor, dp)),
        check_vma=False,
    )
```

profile of v0, /device:TPU:8, one launch (start us, length us, event | category | flops | bytes accessed | tf_op | source)
XLA Modules:
  0.0 241.7 jit_solution(16387781204282420126)
XLA Ops:
  0.6 3.1 %collective-permute-start.4 = (bf16[24,2048]{1,0:T(8,128)(2,1)}, bf16[24,2048]{1,0:T(8,128)(2,1)S(1)}, u32[]{:S(2)}, u32[]{:S(2)}) collective-permute-start(bf16[24,2048]{1,0:T(8,128)(2,1)} %param.10), channel_id=1, source_target_pairs={{0,1},{1,0},{2,3},{3,2},{4,5},{5,4},{6,7},{7,6},{8,9},{9,8},{10,11... | collective-permute-start | bytes 294920 | tf_op jit(solution)/shard_map/ppermute | solution.py:17
  3.8 3.3 %collective-permute-done.4 = bf16[24,2048]{1,0:T(8,128)(2,1)S(1)} collective-permute-done((bf16[24,2048]{1,0:T(8,128)(2,1)}, bf16[24,2048]{1,0:T(8,128)(2,1)S(1)}, u32[]{:S(2)}, u32[]{:S(2)}) %collective-permute-start.4) | collective-permute-done | bytes 98336 | tf_op jit(solution)/shard_map/ppermute | solution.py:17
  8.2 1.7 collective-permute-start.5
  11.9 7.1 %all-to-all-start.1 = ((bf16[8,64,344]{2,1,0:T(8,128)(2,1)}), bf16[8,64,344]{2,1,0:T(8,128)(2,1)S(1)}, u32[]{:S(2)}, u32[]{:S(2)}) async-start(bf16[8,64,344]{2,1,0:T(8,128)(2,1)} %broadcast_in_dim.37), calls=%async_computation.1 | async-start | bytes 786432 | tf_op jit(solution)/shard_map/all_to_all | solution.py:51
  19.1 2.8 %collective-permute-start.7 = (bf16[48,2048]{1,0:T(8,128)(2,1)S(1)}, bf16[48,2048]{1,0:T(8,128)(2,1)S(1)}, u32[]{:S(2)}, u32[]{:S(2)}) collective-permute-start(bf16[48,2048]{1,0:T(8,128)(2,1)S(1)} %get-tuple-element.305), channel_id=1, source_target_pairs={{0,4},{2,6},{4,0},{6,2},{1,5},{3,7},{5,1},{7,3},{8,12},{10,14},{12... | collective-permute-start | bytes 589832 | tf_op jit(solution)/shard_map/ppermute | solution.py:17
  21.9 7.9 %collective-permute-done.6 = bf16[48,2048]{1,0:T(8,128)(2,1)S(1)} collective-permute-done((bf16[48,2048]{1,0:T(8,128)(2,1)S(1)}, bf16[48,2048]{1,0:T(8,128)(2,1)S(1)}, u32[]{:S(2)}, u32[]{:S(2)}) %collective-permute-start.6) | collective-permute-done | bytes 196640 | tf_op jit(solution)/shard_map/ppermute | solution.py:17
  29.9 2.7 %collective-permute-done.7 = bf16[48,2048]{1,0:T(8,128)(2,1)S(1)} collective-permute-done((bf16[48,2048]{1,0:T(8,128)(2,1)S(1)}, bf16[48,2048]{1,0:T(8,128)(2,1)S(1)}, u32[]{:S(2)}, u32[]{:S(2)}) %collective-permute-start.7) | collective-permute-done | bytes 196640 | tf_op jit(solution)/shard_map/ppermute | solution.py:17
  34.2 7.7 %collective-permute-start.15 = (bf16[2,86,128]{2,1,0:T(8,128)(2,1)S(1)}, bf16[2,86,128]{2,1,0:T(8,128)(2,1)S(1)}, u32[]{:S(2)}, u32[]{:S(2)}) collective-permute-start(bf16[2,86,128]{2,1,0:T(8,128)(2,1)S(1)} %bitcast.203), channel_id=1, source_target_pairs={{0,0},{1,32},{2,64},{3,96},{4,128},{5,160},{6,192},{7,224},{8,8},{... | collective-permute-start | bytes 132104 | tf_op jit(solution)/shard_map/ppermute | solution.py:140
  43.1 5.3 %all-to-all-start = ((bf16[16,192,128]{2,1,0:T(8,128)(2,1)}), bf16[16,192,128]{2,1,0:T(8,128)(2,1)S(1)}, u32[]{:S(2)}, u32[]{:S(2)}) async-start(bf16[16,192,128]{2,1,0:T(8,128)(2,1)} %broadcast_in_dim.36), calls=%async_computation | async-start | bytes 1572864 | tf_op jit(solution)/shard_map/all_to_all | solution.py:51
  49.0 3.3 %fusion.5 = bf16[688,64]{0,1:T(8,128)(2,1)S(1)} fusion(bf16[64,2752]{1,0:T(8,128)(2,1)S(1)} %reshape.204, bf16[688,2752]{1,0:T(8,128)(2,1)} %param.15), kind=kOutput, calls=%fused_computation.20 | convolution fusion | flops 242396160 | bytes 4227072 | tf_op jit(solution)/shard_map/dot_general | solution.py:13
  56.2 3.0 %collective-permute-done.12 = bf16[2,172,64]{2,1,0:T(8,128)(2,1)S(1)} collective-permute-done((bf16[2,172,64]{2,1,0:T(8,128)(2,1)S(1)}, bf16[2,172,64]{2,1,0:T(8,128)(2,1)S(1)}, u32[]{:S(2)}, u32[]{:S(2)}) %collective-permute-start.12) | collective-permute-done | bytes 44064 | tf_op jit(solution)/shard_map/ppermute | solution.py:17
  63.3 6.9 %all-to-all-start.6 = ((bf16[16,2,86,128]{3,1,2,0:T(2,128)(2,1)}), bf16[16,2,86,128]{3,1,2,0:T(2,128)(2,1)}, u32[]{:S(2)}, u32[]{:S(2)}) async-start(bf16[16,2,86,128]{3,1,2,0:T(2,128)(2,1)} %broadcast_in_dim.94), calls=%async_computation.6 | async-start | bytes 1409024 | tf_op jit(solution)/shard_map/all_to_all | solution.py:51
  71.9 27.3 %while.38 = (s32[]{:T(128)}, bf16[1,344,128]{2,1,0:T(8,128)(2,1)S(1)}, bf16[1,344,128]{2,1,0:T(8,128)(2,1)S(1)}, bf16[8,344,128]{2,1,0:T(8,128)(2,1)S(1)}, s32[]...) while((s32[]{:T(128)}, bf16[1,344,128]{2,1,0:T(8,128)(2,1)S(1)}, ...), condition=%wide.region_1.2_spmd, body=%wide.region_0.1_spmd.sunk | while | flops 12 | bytes 1409329 | solution.py:68
  73.0 2.1 collective-permute-start.1
  75.1 3.2 %collective-permute-done = bf16[1,344,128]{2,1,0:T(8,128)(2,1)S(1)} collective-permute-done((bf16[1,344,128]{2,1,0:T(8,128)(2,1)S(1)}, bf16[1,344,128]{2,1,0:T(8,128)(2,1)S(1)}, u32[]{:S(2)}, u32[]{:S(2)}) %collective-permute-start) | collective-permute-done | bytes 88096 | tf_op jit(solution)/shard_map/while/body/eval_jaxpr/ppermute | solution.py:17
  78.3 1.7 collective-permute-done.1
  80.1 2.0 collective-permute-start
  83.4 2.5 %collective-permute-done = bf16[1,344,128]{2,1,0:T(8,128)(2,1)S(1)} collective-permute-done((bf16[1,344,128]{2,1,0:T(8,128)(2,1)S(1)}, bf16[1,344,128]{2,1,0:T(8,128)(2,1)S(1)}, u32[]{:S(2)}, u32[]{:S(2)}) %collective-permute-start) | collective-permute-done | bytes 88096 | tf_op jit(solution)/shard_map/while/body/eval_jaxpr/ppermute | solution.py:17
  86.6 1.8 collective-permute-start
  90.0 2.5 %collective-permute-done = bf16[1,344,128]{2,1,0:T(8,128)(2,1)S(1)} collective-permute-done((bf16[1,344,128]{2,1,0:T(8,128)(2,1)S(1)}, bf16[1,344,128]{2,1,0:T(8,128)(2,1)S(1)}, u32[]{:S(2)}, u32[]{:S(2)}) %collective-permute-start) | collective-permute-done | bytes 88096 | tf_op jit(solution)/shard_map/while/body/eval_jaxpr/ppermute | solution.py:17
  94.6 1.7 collective-permute-start.1
  96.4 2.5 %collective-permute-done = bf16[1,344,128]{2,1,0:T(8,128)(2,1)S(1)} collective-permute-done((bf16[1,344,128]{2,1,0:T(8,128)(2,1)S(1)}, bf16[1,344,128]{2,1,0:T(8,128)(2,1)S(1)}, u32[]{:S(2)}, u32[]{:S(2)}) %collective-permute-start) | collective-permute-done | bytes 88096 | tf_op jit(solution)/shard_map/while/body/eval_jaxpr/ppermute | solution.py:17
  103.8 1.8 reshape.217
  114.3 4.3 %all-to-all-start.4 = ((bf16[8,2,64,344]{3,2,1,0:T(8,128)(2,1)}), bf16[8,2,64,344]{3,2,1,0:T(8,128)(2,1)}, u32[]{:S(2)}, u32[]{:S(2)}) async-start(bf16[8,2,64,344]{3,2,1,0:T(8,128)(2,1)} %copy.149), calls=%async_computation.4 | async-start | bytes 1572864 | tf_op jit(solution)/shard_map/all_to_all | solution.py:51
  118.6 1.8 convolution_convert_fusion.1
  125.4 2.3 reshape.215
  127.7 2.6 %copy.163 = bf16[4,86,1024]{2,0,1:T(4,128)(2,1)} copy(bf16[4,86,1024]{2,1,0:T(8,128)(2,1)} %reshape.215) | data formatting | bytes 1409024 | tf_op jit(solution)/shard_map/reshape | solution.py:141
  130.8 2.0 add_convert_fusion
  133.8 4.4 %all-to-all-done.4 = bf16[8,2,64,344]{3,2,1,0:T(8,128)(2,1)} async-done(((bf16[8,2,64,344]{3,2,1,0:T(8,128)(2,1)}), bf16[8,2,64,344]{3,2,1,0:T(8,128)(2,1)}, u32[]{:S(2)}, u32[]{:S(2)}) %all-to-all-start.4) | async-done | bytes 704544 | tf_op jit(solution)/shard_map/all_to_all | solution.py:51
  138.2 7.4 %all-to-all-start.2 = ((bf16[16,192,128]{2,1,0:T(8,128)(2,1)}), bf16[16,192,128]{2,1,0:T(8,128)(2,1)S(1)}, u32[]{:S(2)}, u32[]{:S(2)}) async-start(bf16[16,192,128]{2,1,0:T(8,128)(2,1)} %bitcast.32), calls=%async_computation.2 | async-start | bytes 1572864 | tf_op jit(solution)/shard_map/all_to_all | solution.py:51
  148.6 31.9 %while.39 = (s32[]{:T(128)}, bf16[1,2,64,344]{3,2,1,0:T(8,128)(2,1)S(1)}, bf16[1,2,64,344]{3,2,1,0:T(8,128)(2,1)}, bf16[8,2,64,344]{3,2,1,0:T(8,128)(2,1)}, s32[...) while((s32[]{:T(128)}, bf16[1,2,64,344]{3,2,1,0:T(8,128)(2,1)S(1)}, ...), condition=%wide.region_7.8_spmd, body=%wide.region_6.7_spmd.sunk | while | flops 12 | bytes 1429809 | solution.py:68
  149.1 2.7 %collective-permute-start.3 = (bf16[1,2,64,344]{3,2,1,0:T(8,128)(2,1)}, bf16[1,2,64,344]{3,2,1,0:T(8,128)(2,1)S(1)}, u32[]{:S(2)}, u32[]{:S(2)}) collective-permute-start(bf16[1,2,64,344]{3,2,1,0:T(8,128)(2,1)} %get-tuple-element.462), channel_id=1, source_target_pairs={{0,112},{16,0},{32,16},{48,32},{64,48},{80,64},{96,80},{112,96},{1... | collective-permute-start | bytes 264200 | tf_op jit(solution)/shard_map/while/body/eval_jaxpr/ppermute | solution.py:17
  151.8 2.6 %collective-permute-done.2 = bf16[1,2,64,344]{3,2,1,0:T(8,128)(2,1)S(1)} collective-permute-done((bf16[1,2,64,344]{3,2,1,0:T(8,128)(2,1)S(1)}, bf16[1,2,64,344]{3,2,1,0:T(8,128)(2,1)S(1)}, u32[]{:S(2)}, u32[]{:S(2)}) %collective-permute-start.2) | collective-permute-done | bytes 88096 | tf_op jit(solution)/shard_map/while/body/eval_jaxpr/ppermute | solution.py:17
  156.4 3.4 %collective-permute-start.3 = (bf16[1,2,64,344]{3,2,1,0:T(8,128)(2,1)}, bf16[1,2,64,344]{3,2,1,0:T(8,128)(2,1)S(1)}, u32[]{:S(2)}, u32[]{:S(2)}) collective-permute-start(bf16[1,2,64,344]{3,2,1,0:T(8,128)(2,1)} %get-tuple-element.462), channel_id=1, source_target_pairs={{0,112},{16,0},{32,16},{48,32},{64,48},{80,64},{96,80},{112,96},{1... | collective-permute-start | bytes 264200 | tf_op jit(solution)/shard_map/while/body/eval_jaxpr/ppermute | solution.py:17
  159.8 2.6 %collective-permute-done.2 = bf16[1,2,64,344]{3,2,1,0:T(8,128)(2,1)S(1)} collective-permute-done((bf16[1,2,64,344]{3,2,1,0:T(8,128)(2,1)S(1)}, bf16[1,2,64,344]{3,2,1,0:T(8,128)(2,1)S(1)}, u32[]{:S(2)}, u32[]{:S(2)}) %collective-permute-start.2) | collective-permute-done | bytes 88096 | tf_op jit(solution)/shard_map/while/body/eval_jaxpr/ppermute | solution.py:17
  164.5 3.4 %collective-permute-start.3 = (bf16[1,2,64,344]{3,2,1,0:T(8,128)(2,1)}, bf16[1,2,64,344]{3,2,1,0:T(8,128)(2,1)S(1)}, u32[]{:S(2)}, u32[]{:S(2)}) collective-permute-start(bf16[1,2,64,344]{3,2,1,0:T(8,128)(2,1)} %get-tuple-element.462), channel_id=1, source_target_pairs={{0,112},{16,0},{32,16},{48,32},{64,48},{80,64},{96,80},{112,96},{1... | collective-permute-start | bytes 264200 | tf_op jit(solution)/shard_map/while/body/eval_jaxpr/ppermute | solution.py:17
  168.0 2.6 %collective-permute-done.2 = bf16[1,2,64,344]{3,2,1,0:T(8,128)(2,1)S(1)} collective-permute-done((bf16[1,2,64,344]{3,2,1,0:T(8,128)(2,1)S(1)}, bf16[1,2,64,344]{3,2,1,0:T(8,128)(2,1)S(1)}, u32[]{:S(2)}, u32[]{:S(2)}) %collective-permute-start.2) | collective-permute-done | bytes 88096 | tf_op jit(solution)/shard_map/while/body/eval_jaxpr/ppermute | solution.py:17
  173.4 2.6 %collective-permute-start.3 = (bf16[1,2,64,344]{3,2,1,0:T(8,128)(2,1)}, bf16[1,2,64,344]{3,2,1,0:T(8,128)(2,1)S(1)}, u32[]{:S(2)}, u32[]{:S(2)}) collective-permute-start(bf16[1,2,64,344]{3,2,1,0:T(8,128)(2,1)} %get-tuple-element.462), channel_id=1, source_target_pairs={{0,112},{16,0},{32,16},{48,32},{64,48},{80,64},{96,80},{112,96},{1... | collective-permute-start | bytes 264200 | tf_op jit(solution)/shard_map/while/body/eval_jaxpr/ppermute | solution.py:17
  176.0 2.6 %collective-permute-done.2 = bf16[1,2,64,344]{3,2,1,0:T(8,128)(2,1)S(1)} collective-permute-done((bf16[1,2,64,344]{3,2,1,0:T(8,128)(2,1)S(1)}, bf16[1,2,64,344]{3,2,1,0:T(8,128)(2,1)S(1)}, u32[]{:S(2)}, u32[]{:S(2)}) %collective-permute-start.2) | collective-permute-done | bytes 88096 | tf_op jit(solution)/shard_map/while/body/eval_jaxpr/ppermute | solution.py:17
  184.8 2.0 copy.159
  189.3 1.7 fusion.15
  191.0 1.9 fusion.4
  194.4 7.5 %all-to-all-start.3 = ((bf16[32,64,128]{2,1,0:T(8,128)(2,1)}), bf16[32,64,128]{2,1,0:T(8,128)(2,1)}, u32[]{:S(2)}, u32[]{:S(2)}) async-start(bf16[32,64,128]{2,1,0:T(8,128)(2,1)} %bitcast.33), calls=%async_computation.3 | async-start | bytes 1048576 | tf_op jit(solution)/shard_map/all_to_all | solution.py:51
  203.3 1.7 add_convert_fusion.1
  206.4 13.8 %all-to-all-done.3 = bf16[32,64,128]{2,1,0:T(8,128)(2,1)} async-done(((bf16[32,64,128]{2,1,0:T(8,128)(2,1)}), bf16[32,64,128]{2,1,0:T(8,128)(2,1)}, u32[]{:S(2)}, u32[]{:S(2)}) %all-to-all-start.3) | async-done | bytes 524320 | tf_op jit(solution)/shard_map/all_to_all | solution.py:51
  220.2 7.2 %all-to-all-start.5 = ((bf16[16,64,344]{2,1,0:T(8,128)(2,1)}), bf16[16,64,344]{2,1,0:T(8,128)(2,1)S(1)}, u32[]{:S(2)}, u32[]{:S(2)}) async-start(bf16[16,64,344]{2,1,0:T(8,128)(2,1)} %bitcast.52), calls=%async_computation.5 | async-start | bytes 1572864 | tf_op jit(solution)/shard_map/all_to_all | solution.py:51
  229.0 9.2 %collective-permute-done.18 = bf16[2,172,86]{2,1,0:T(8,128)(2,1)S(1)} collective-permute-done((bf16[2,172,86]{2,1,0:T(8,128)(2,1)S(1)}, bf16[2,172,86]{2,1,0:T(8,128)(2,1)S(1)}, u32[]{:S(2)}, u32[]{:S(2)}) %collective-permute-start.18) | collective-permute-done | bytes 59200 | tf_op jit(solution)/shard_map/ppermute | solution.py:17
  239.2 1.7 convert_reduce_fusion.1
  (196 shorter events, 69.4 us)
Async XLA Ops:
  0.6 32.0 %copy-start = (bf16[2048,128]{1,0:T(8,128)(2,1)S(1)}, bf16[2048,128]{1,0:T(8,128)(2,1)}, u32[]{:S(2)}) copy-start(bf16[2048,128]{1,0:T(8,128)(2,1)} %param.12) | copy-start | bytes 1572868
  0.6 6.4 %collective-permute-start.4 = (bf16[24,2048]{1,0:T(8,128)(2,1)}, bf16[24,2048]{1,0:T(8,128)(2,1)S(1)}, u32[]{:S(2)}, u32[]{:S(2)}) collective-permute-start(bf16[24,2048]{1,0:T(8,128)(2,1)} %param.10), channel_id=1, source_target_pairs={{0,1},{1,0},{2,3},{3,2},{4,5},{5,4},{6,7},{7,6},{8,9},{9,8},{10,11... | collective-permute-start | bytes 294920 | tf_op jit(solution)/shard_map/ppermute | solution.py:17
  8.2 13.7 %collective-permute-start.5 = (bf16[48,2048]{1,0:T(8,128)(2,1)S(1)}, bf16[48,2048]{1,0:T(8,128)(2,1)S(1)}, u32[]{:S(2)}, u32[]{:S(2)}) collective-permute-start(bf16[48,2048]{1,0:T(8,128)(2,1)S(1)} %get-tuple-element.305), channel_id=1, source_target_pairs={{0,2},{2,4},{4,6},{6,0},{1,3},{3,5},{5,7},{7,1},{8,10},{10,12},{12... | collective-permute-start | bytes 589832 | tf_op jit(solution)/shard_map/ppermute | solution.py:17
  11.9 30.1 %all-to-all-start.1 = ((bf16[8,64,344]{2,1,0:T(8,128)(2,1)}), bf16[8,64,344]{2,1,0:T(8,128)(2,1)S(1)}, u32[]{:S(2)}, u32[]{:S(2)}) async-start(bf16[8,64,344]{2,1,0:T(8,128)(2,1)} %broadcast_in_dim.37), calls=%async_computation.1 | async-start | bytes 786432 | tf_op jit(solution)/shard_map/all_to_all | solution.py:51
  19.0 15.1 %copy-start.10 = (bf16[192,688]{1,0:T(8,128)(2,1)S(1)}, bf16[192,688]{1,0:T(8,128)(2,1)}, u32[]{:S(2)}) copy-start(bf16[192,688]{1,0:T(8,128)(2,1)} %param.11) | copy-start | bytes 792580
  19.0 10.9 %collective-permute-start.6 = (bf16[48,2048]{1,0:T(8,128)(2,1)S(1)}, bf16[48,2048]{1,0:T(8,128)(2,1)S(1)}, u32[]{:S(2)}, u32[]{:S(2)}) collective-permute-start(bf16[48,2048]{1,0:T(8,128)(2,1)S(1)} %get-tuple-element.305), channel_id=1, source_target_pairs={{0,6},{2,0},{4,2},{6,4},{1,7},{3,1},{5,3},{7,5},{8,14},{10,8},{12,... | collective-permute-start | bytes 589832 | tf_op jit(solution)/shard_map/ppermute | solution.py:17
  19.1 13.6 %collective-permute-start.7 = (bf16[48,2048]{1,0:T(8,128)(2,1)S(1)}, bf16[48,2048]{1,0:T(8,128)(2,1)S(1)}, u32[]{:S(2)}, u32[]{:S(2)}) collective-permute-start(bf16[48,2048]{1,0:T(8,128)(2,1)S(1)} %get-tuple-element.305), channel_id=1, source_target_pairs={{0,4},{2,6},{4,0},{6,2},{1,5},{3,7},{5,1},{7,3},{8,12},{10,14},{12... | collective-permute-start | bytes 589832 | tf_op jit(solution)/shard_map/ppermute | solution.py:17
  34.2 21.9 %collective-permute-start.15 = (bf16[2,86,128]{2,1,0:T(8,128)(2,1)S(1)}, bf16[2,86,128]{2,1,0:T(8,128)(2,1)S(1)}, u32[]{:S(2)}, u32[]{:S(2)}) collective-permute-start(bf16[2,86,128]{2,1,0:T(8,128)(2,1)S(1)} %bitcast.203), channel_id=1, source_target_pairs={{0,0},{1,32},{2,64},{3,96},{4,128},{5,160},{6,192},{7,224},{8,8},{... | collective-permute-start | bytes 132104 | tf_op jit(solution)/shard_map/ppermute | solution.py:140
  43.1 19.0 %all-to-all-start = ((bf16[16,192,128]{2,1,0:T(8,128)(2,1)}), bf16[16,192,128]{2,1,0:T(8,128)(2,1)S(1)}, u32[]{:S(2)}, u32[]{:S(2)}) async-start(bf16[16,192,128]{2,1,0:T(8,128)(2,1)} %broadcast_in_dim.36), calls=%async_computation | async-start | bytes 1572864 | tf_op jit(solution)/shard_map/all_to_all | solution.py:51
  53.0 1.4 collective-permute-start.11
  54.5 4.8 %collective-permute-start.12 = (bf16[2,172,64]{2,1,0:T(8,128)(2,1)S(1)}, bf16[2,172,64]{2,1,0:T(8,128)(2,1)S(1)}, u32[]{:S(2)}, u32[]{:S(2)}) collective-permute-start(bf16[2,172,64]{2,1,0:T(8,128)(2,1)S(1)} %get-tuple-element.329), channel_id=1, source_target_pairs={{0,128},{128,0},{1,129},{129,1},{2,130},{130,2},{3,131},{131,3},{4... | collective-permute-start | bytes 132104 | tf_op jit(solution)/shard_map/ppermute | solution.py:17
  56.1 3.7 %collective-permute-start.8 = (bf16[2,192,172]{1,2,0:T(8,128)(2,1)S(1)}, bf16[2,192,172]{1,2,0:T(8,128)(2,1)S(1)}, u32[]{:S(2)}, u32[]{:S(2)}) collective-permute-start(bf16[2,192,172]{1,2,0:T(8,128)(2,1)S(1)} %get-tuple-element.315), channel_id=1, source_target_pairs={{0,8},{8,0},{1,9},{9,1},{2,10},{10,2},{3,11},{11,3},{4,12},{12,4},... | collective-permute-start | bytes 396296 | tf_op jit(solution)/shard_map/ppermute | solution.py:17
  60.6 40.6 %collective-permute-start.9 = (bf16[2,192,172]{1,2,0:T(8,128)(2,1)S(1)}, bf16[2,192,172]{1,2,0:T(8,128)(2,1)}, u32[]{:S(2)}, u32[]{:S(2)}) collective-permute-start(bf16[2,192,172]{1,2,0:T(8,128)(2,1)S(1)} %get-tuple-element.313), channel_id=1, source_target_pairs={{0,128},{128,0},{1,129},{129,1},{2,130},{130,2},{3,131},{131,3},{4... | collective-permute-start | bytes 396296 | tf_op jit(solution)/shard_map/ppermute | solution.py:17
  63.3 51.1 %all-to-all-start.6 = ((bf16[16,2,86,128]{3,1,2,0:T(2,128)(2,1)}), bf16[16,2,86,128]{3,1,2,0:T(2,128)(2,1)}, u32[]{:S(2)}, u32[]{:S(2)}) async-start(bf16[16,2,86,128]{3,1,2,0:T(2,128)(2,1)} %broadcast_in_dim.94), calls=%async_computation.6 | async-start | bytes 1409024 | tf_op jit(solution)/shard_map/all_to_all | solution.py:51
  71.8 34.0 %collective-permute-start.10 = (bf16[384,1024]{1,0:T(8,128)(2,1)}, bf16[384,1024]{1,0:T(8,128)(2,1)}, u32[]{:S(2)}, u32[]{:S(2)}) collective-permute-start(bf16[384,1024]{1,0:T(8,128)(2,1)} %bitcast.173), channel_id=1, source_target_pairs={{0,8},{8,0},{1,9},{9,1},{2,10},{10,2},{3,11},{11,3},{4,12},{12,4},... | collective-permute-start | bytes 2359304 | tf_op jit(solution)/shard_map/ppermute | solution.py:17
  71.9 6.4 %collective-permute-start = (bf16[1,344,128]{2,1,0:T(8,128)(2,1)S(1)}, bf16[1,344,128]{2,1,0:T(8,128)(2,1)S(1)}, u32[]{:S(2)}, u32[]{:S(2)}) collective-permute-start(bf16[1,344,128]{2,1,0:T(8,128)(2,1)S(1)} %get-tuple-element.431), channel_id=1, source_target_pairs={{0,16},{16,32},{32,48},{48,64},{64,80},{80,96},{96,112},{112,0},{1... | collective-permute-start | bytes 264200 | tf_op jit(solution)/shard_map/while/body/eval_jaxpr/ppermute | solution.py:17
  73.0 7.0 %collective-permute-start.1 = (bf16[1,344,128]{2,1,0:T(8,128)(2,1)S(1)}, bf16[1,344,128]{2,1,0:T(8,128)(2,1)S(1)}, u32[]{:S(2)}, u32[]{:S(2)}) collective-permute-start(bf16[1,344,128]{2,1,0:T(8,128)(2,1)S(1)} %get-tuple-element.432), channel_id=1, source_target_pairs={{0,112},{16,0},{32,16},{48,32},{64,48},{80,64},{96,80},{112,96},{1... | collective-permute-start | bytes 264200 | tf_op jit(solution)/shard_map/while/body/eval_jaxpr/ppermute | solution.py:17
  80.1 5.8 %collective-permute-start = (bf16[1,344,128]{2,1,0:T(8,128)(2,1)S(1)}, bf16[1,344,128]{2,1,0:T(8,128)(2,1)S(1)}, u32[]{:S(2)}, u32[]{:S(2)}) collective-permute-start(bf16[1,344,128]{2,1,0:T(8,128)(2,1)S(1)} %get-tuple-element.431), channel_id=1, source_target_pairs={{0,16},{16,32},{32,48},{48,64},{64,80},{80,96},{96,112},{112,0},{1... | collective-permute-start | bytes 264200 | tf_op jit(solution)/shard_map/while/body/eval_jaxpr/ppermute | solution.py:17
  82.1 4.5 %collective-permute-start.1 = (bf16[1,344,128]{2,1,0:T(8,128)(2,1)S(1)}, bf16[1,344,128]{2,1,0:T(8,128)(2,1)S(1)}, u32[]{:S(2)}, u32[]{:S(2)}) collective-permute-start(bf16[1,344,128]{2,1,0:T(8,128)(2,1)S(1)} %get-tuple-element.432), channel_id=1, source_target_pairs={{0,112},{16,0},{32,16},{48,32},{64,48},{80,64},{96,80},{112,96},{1... | collective-permute-start | bytes 264200 | tf_op jit(solution)/shard_map/while/body/eval_jaxpr/ppermute | solution.py:17
  86.6 5.8 %collective-permute-start = (bf16[1,344,128]{2,1,0:T(8,128)(2,1)S(1)}, bf16[1,344,128]{2,1,0:T(8,128)(2,1)S(1)}, u32[]{:S(2)}, u32[]{:S(2)}) collective-permute-start(bf16[1,344,128]{2,1,0:T(8,128)(2,1)S(1)} %get-tuple-element.431), channel_id=1, source_target_pairs={{0,16},{16,32},{32,48},{48,64},{64,80},{80,96},{96,112},{112,0},{1... | collective-permute-start | bytes 264200 | tf_op jit(solution)/shard_map/while/body/eval_jaxpr/ppermute | solution.py:17
  88.5 4.5 %collective-permute-start.1 = (bf16[1,344,128]{2,1,0:T(8,128)(2,1)S(1)}, bf16[1,344,128]{2,1,0:T(8,128)(2,1)S(1)}, u32[]{:S(2)}, u32[]{:S(2)}) collective-permute-start(bf16[1,344,128]{2,1,0:T(8,128)(2,1)S(1)} %get-tuple-element.432), channel_id=1, source_target_pairs={{0,112},{16,0},{32,16},{48,32},{64,48},{80,64},{96,80},{112,96},{1... | collective-permute-start | bytes 264200 | tf_op jit(solution)/shard_map/while/body/eval_jaxpr/ppermute | solution.py:17
  93.0 5.8 %collective-permute-start = (bf16[1,344,128]{2,1,0:T(8,128)(2,1)S(1)}, bf16[1,344,128]{2,1,0:T(8,128)(2,1)S(1)}, u32[]{:S(2)}, u32[]{:S(2)}) collective-permute-start(bf16[1,344,128]{2,1,0:T(8,128)(2,1)S(1)} %get-tuple-element.431), channel_id=1, source_target_pairs={{0,16},{16,32},{32,48},{48,64},{64,80},{80,96},{96,112},{112,0},{1... | collective-permute-start | bytes 264200 | tf_op jit(solution)/shard_map/while/body/eval_jaxpr/ppermute | solution.py:17
  94.6 4.5 %collective-permute-start.1 = (bf16[1,344,128]{2,1,0:T(8,128)(2,1)S(1)}, bf16[1,344,128]{2,1,0:T(8,128)(2,1)S(1)}, u32[]{:S(2)}, u32[]{:S(2)}) collective-permute-start(bf16[1,344,128]{2,1,0:T(8,128)(2,1)S(1)} %get-tuple-element.432), channel_id=1, source_target_pairs={{0,112},{16,0},{32,16},{48,32},{64,48},{80,64},{96,80},{112,96},{1... | collective-permute-start | bytes 264200 | tf_op jit(solution)/shard_map/while/body/eval_jaxpr/ppermute | solution.py:17
  99.2 19.4 %copy-start.4 = (bf16[8,344,128]{2,1,0:T(8,128)(2,1)}, bf16[8,344,128]{2,1,0:T(8,128)(2,1)S(1)}, u32[]{:S(2)}) copy-start(bf16[8,344,128]{2,1,0:T(8,128)(2,1)S(1)} %get-tuple-element.275) | copy-start | bytes 2113540
  111.1 2.5 %copy-start.12 = (bf16[768,172]{0,1:T(8,128)(2,1)S(1)}, bf16[768,172]{0,1:T(8,128)(2,1)}, u32[]{:S(2)}) copy-start(bf16[768,172]{0,1:T(8,128)(2,1)} %copy-done.11) | copy-start | bytes 792580
  111.1 2.5 %copy-start.14 = (bf16[768,172]{0,1:T(8,128)(2,1)S(1)}, bf16[768,172]{0,1:T(8,128)(2,1)}, u32[]{:S(2)}) copy-start(bf16[768,172]{0,1:T(8,128)(2,1)} %copy-done.13) | copy-start | bytes 792580
  114.3 23.9 %all-to-all-start.4 = ((bf16[8,2,64,344]{3,2,1,0:T(8,128)(2,1)}), bf16[8,2,64,344]{3,2,1,0:T(8,128)(2,1)}, u32[]{:S(2)}, u32[]{:S(2)}) async-start(bf16[8,2,64,344]{3,2,1,0:T(8,128)(2,1)} %copy.149), calls=%async_computation.4 | async-start | bytes 1572864 | tf_op jit(solution)/shard_map/all_to_all | solution.py:51
  120.4 10.4 %collective-permute-start.13 = (bf16[8,384,128]{2,1,0:T(8,128)(2,1)}, bf16[8,384,128]{2,1,0:T(8,128)(2,1)}, u32[]{:S(2)}, u32[]{:S(2)}) collective-permute-start(bf16[8,384,128]{2,1,0:T(8,128)(2,1)} %convolution_convert_fusion.1), channel_id=1, source_target_pairs={{0,8},{8,0},{1,9},{9,1},{2,10},{10,2},{3,11},{11,3},{4,12},{12,4},... | collective-permute-start | bytes 2359304 | tf_op jit(solution)/shard_map/ppermute | solution.py:17
  125.4 5.4 %copy-start.5 = (bf16[8,344,128]{2,1,0:T(8,128)(2,1)S(1)}, bf16[8,344,128]{2,1,0:T(8,128)(2,1)}, u32[]{:S(2)}) copy-start(bf16[8,344,128]{2,1,0:T(8,128)(2,1)} %copy-done.4) | copy-start | bytes 2113540
  125.4 5.4 %copy-start.16 = (bf16[384,344]{0,1:T(8,128)(2,1)S(1)}, bf16[384,344]{0,1:T(8,128)(2,1)}, u32[]{:S(2)}) copy-start(bf16[384,344]{0,1:T(8,128)(2,1)} %get-tuple-element.310) | copy-start | bytes 792580
  130.3 59.0 %collective-permute-start.16 = (bf16[4,86,1024]{2,0,1:T(4,128)(2,1)}, bf16[4,86,1024]{2,0,1:T(4,128)(2,1)}, u32[]{:S(2)}, u32[]{:S(2)}) collective-permute-start(bf16[4,86,1024]{2,0,1:T(4,128)(2,1)} %copy.163), channel_id=1, source_target_pairs={{0,8},{8,0},{1,9},{9,1},{2,10},{10,2},{3,11},{11,3},{4,12},{12,4},... | collective-permute-start | bytes 2113544 | tf_op jit(solution)/shard_map/ppermute | solution.py:17
  138.2 54.7 %all-to-all-start.2 = ((bf16[16,192,128]{2,1,0:T(8,128)(2,1)}), bf16[16,192,128]{2,1,0:T(8,128)(2,1)S(1)}, u32[]{:S(2)}, u32[]{:S(2)}) async-start(bf16[16,192,128]{2,1,0:T(8,128)(2,1)} %bitcast.32), calls=%async_computation.2 | async-start | bytes 1572864 | tf_op jit(solution)/shard_map/all_to_all | solution.py:51
  148.6 5.8 %collective-permute-start.2 = (bf16[1,2,64,344]{3,2,1,0:T(8,128)(2,1)S(1)}, bf16[1,2,64,344]{3,2,1,0:T(8,128)(2,1)S(1)}, u32[]{:S(2)}, u32[]{:S(2)}) collective-permute-start(bf16[1,2,64,344]{3,2,1,0:T(8,128)(2,1)S(1)} %get-tuple-element.461), channel_id=1, source_target_pairs={{0,16},{16,32},{32,48},{48,64},{64,80},{80,96},{96,112},{112,0},{1... | collective-permute-start | bytes 264200 | tf_op jit(solution)/shard_map/while/body/eval_jaxpr/ppermute | solution.py:17
  149.1 5.3 %collective-permute-start.3 = (bf16[1,2,64,344]{3,2,1,0:T(8,128)(2,1)}, bf16[1,2,64,344]{3,2,1,0:T(8,128)(2,1)S(1)}, u32[]{:S(2)}, u32[]{:S(2)}) collective-permute-start(bf16[1,2,64,344]{3,2,1,0:T(8,128)(2,1)} %get-tuple-element.462), channel_id=1, source_target_pairs={{0,112},{16,0},{32,16},{48,32},{64,48},{80,64},{96,80},{112,96},{1... | collective-permute-start | bytes 264200 | tf_op jit(solution)/shard_map/while/body/eval_jaxpr/ppermute | solution.py:17
  156.4 6.0 %collective-permute-start.2 = (bf16[1,2,64,344]{3,2,1,0:T(8,128)(2,1)S(1)}, bf16[1,2,64,344]{3,2,1,0:T(8,128)(2,1)S(1)}, u32[]{:S(2)}, u32[]{:S(2)}) collective-permute-start(bf16[1,2,64,344]{3,2,1,0:T(8,128)(2,1)S(1)} %get-tuple-element.461), channel_id=1, source_target_pairs={{0,16},{16,32},{32,48},{48,64},{64,80},{80,96},{96,112},{112,0},{1... | collective-permute-start | bytes 264200 | tf_op jit(solution)/shard_map/while/body/eval_jaxpr/ppermute | solution.py:17
  156.4 6.0 %collective-permute-start.3 = (bf16[1,2,64,344]{3,2,1,0:T(8,128)(2,1)}, bf16[1,2,64,344]{3,2,1,0:T(8,128)(2,1)S(1)}, u32[]{:S(2)}, u32[]{:S(2)}) collective-permute-start(bf16[1,2,64,344]{3,2,1,0:T(8,128)(2,1)} %get-tuple-element.462), channel_id=1, source_target_pairs={{0,112},{16,0},{32,16},{48,32},{64,48},{80,64},{96,80},{112,96},{1... | collective-permute-start | bytes 264200 | tf_op jit(solution)/shard_map/while/body/eval_jaxpr/ppermute | solution.py:17
  164.4 6.2 %collective-permute-start.2 = (bf16[1,2,64,344]{3,2,1,0:T(8,128)(2,1)S(1)}, bf16[1,2,64,344]{3,2,1,0:T(8,128)(2,1)S(1)}, u32[]{:S(2)}, u32[]{:S(2)}) collective-permute-start(bf16[1,2,64,344]{3,2,1,0:T(8,128)(2,1)S(1)} %get-tuple-element.461), channel_id=1, source_target_pairs={{0,16},{16,32},{32,48},{48,64},{64,80},{80,96},{96,112},{112,0},{1... | collective-permute-start | bytes 264200 | tf_op jit(solution)/shard_map/while/body/eval_jaxpr/ppermute | solution.py:17
  164.5 6.0 %collective-permute-start.3 = (bf16[1,2,64,344]{3,2,1,0:T(8,128)(2,1)}, bf16[1,2,64,344]{3,2,1,0:T(8,128)(2,1)S(1)}, u32[]{:S(2)}, u32[]{:S(2)}) collective-permute-start(bf16[1,2,64,344]{3,2,1,0:T(8,128)(2,1)} %get-tuple-element.462), channel_id=1, source_target_pairs={{0,112},{16,0},{32,16},{48,32},{64,48},{80,64},{96,80},{112,96},{1... | collective-permute-start | bytes 264200 | tf_op jit(solution)/shard_map/while/body/eval_jaxpr/ppermute | solution.py:17
  172.5 6.0 %collective-permute-start.2 = (bf16[1,2,64,344]{3,2,1,0:T(8,128)(2,1)S(1)}, bf16[1,2,64,344]{3,2,1,0:T(8,128)(2,1)S(1)}, u32[]{:S(2)}, u32[]{:S(2)}) collective-permute-start(bf16[1,2,64,344]{3,2,1,0:T(8,128)(2,1)S(1)} %get-tuple-element.461), channel_id=1, source_target_pairs={{0,16},{16,32},{32,48},{48,64},{64,80},{80,96},{96,112},{112,0},{1... | collective-permute-start | bytes 264200 | tf_op jit(solution)/shard_map/while/body/eval_jaxpr/ppermute | solution.py:17
  173.4 5.2 %collective-permute-start.3 = (bf16[1,2,64,344]{3,2,1,0:T(8,128)(2,1)}, bf16[1,2,64,344]{3,2,1,0:T(8,128)(2,1)S(1)}, u32[]{:S(2)}, u32[]{:S(2)}) collective-permute-start(bf16[1,2,64,344]{3,2,1,0:T(8,128)(2,1)} %get-tuple-element.462), channel_id=1, source_target_pairs={{0,112},{16,0},{32,16},{48,32},{64,48},{80,64},{96,80},{112,96},{1... | collective-permute-start | bytes 264200 | tf_op jit(solution)/shard_map/while/body/eval_jaxpr/ppermute | solution.py:17
  186.8 2.4 %copy-start.6 = (bf16[4,86,1024]{2,1,0:T(8,128)(2,1)S(1)}, bf16[4,86,1024]{2,1,0:T(8,128)(2,1)}, u32[]{:S(2)}) copy-start(bf16[4,86,1024]{2,1,0:T(8,128)(2,1)} %reshape.215) | copy-start | bytes 2113540
  189.2 1.8 copy-start.7
  189.2 14.1 %collective-permute-start.14 = (bf16[8,128,344]{1,2,0:T(8,128)(2,1)}, bf16[8,128,344]{1,2,0:T(8,128)(2,1)}, u32[]{:S(2)}, u32[]{:S(2)}) collective-permute-start(bf16[8,128,344]{1,2,0:T(8,128)(2,1)} %fusion), channel_id=1, source_target_pairs={{0,8},{8,0},{1,9},{9,1},{2,10},{10,2},{3,11},{11,3},{4,12},{12,4},... | collective-permute-start | bytes 2113544 | tf_op jit(solution)/shard_map/ppermute | solution.py:17
  192.9 9.2 %copy-start.15 = (bf16[2,32,344]{2,1,0:T(8,128)(2,1)S(1)}, bf16[2,32,344]{2,1,0:T(8,128)(2,1)}, u32[]{:S(2)}) copy-start(bf16[2,32,344]{2,1,0:T(8,128)(2,1)} %get-tuple-element.336) | copy-start | bytes 132100
  194.4 25.9 %all-to-all-start.3 = ((bf16[32,64,128]{2,1,0:T(8,128)(2,1)}), bf16[32,64,128]{2,1,0:T(8,128)(2,1)}, u32[]{:S(2)}, u32[]{:S(2)}) async-start(bf16[32,64,128]{2,1,0:T(8,128)(2,1)} %bitcast.33), calls=%async_computation.3 | async-start | bytes 1048576 | tf_op jit(solution)/shard_map/all_to_all | solution.py:51
  201.9 1.4 collective-permute-start.17
  220.2 20.7 %all-to-all-start.5 = ((bf16[16,64,344]{2,1,0:T(8,128)(2,1)}), bf16[16,64,344]{2,1,0:T(8,128)(2,1)S(1)}, u32[]{:S(2)}, u32[]{:S(2)}) async-start(bf16[16,64,344]{2,1,0:T(8,128)(2,1)} %bitcast.52), calls=%async_computation.5 | async-start | bytes 1572864 | tf_op jit(solution)/shard_map/all_to_all | solution.py:51
  227.5 10.7 %collective-permute-start.18 = (bf16[2,172,86]{2,1,0:T(8,128)(2,1)S(1)}, bf16[2,172,86]{2,1,0:T(8,128)(2,1)S(1)}, u32[]{:S(2)}, u32[]{:S(2)}) collective-permute-start(bf16[2,172,86]{2,1,0:T(8,128)(2,1)S(1)} %fusion.30), channel_id=1, source_target_pairs={{0,128},{128,0},{1,129},{129,1},{2,130},{130,2},{3,131},{131,3},{4... | collective-permute-start | bytes 177512 | tf_op jit(solution)/shard_map/ppermute | solution.py:17
  (7 other events, 6.9 us)
where the time goes:
time: 243 us; the launch traced here: 242 us
  starting transfers between devices  93.6 us (39%)
  waiting for transfers between devices  70.8 us (29%)
  local copies, waits for them, and re-layouts  48.4 us (20%)
  matrix products  18.7 us (8%)
  other arithmetic  8.75 us (4%)
    ppermute x30, waiting for transfers between devices, shift(): lax.ppermute(value, axis, [(i, (i + step) % size) for i in range(size)])  52.5 us
    all_to_all x7, starting transfers between devices, exchange(): return lax.all_to_all(pieces, axes, 0, 0, tiled=True)  45.7 us
    ppermute x30, starting transfers between devices, shift(): lax.ppermute(value, axis, [(i, (i + step) % size) for i in range(size)])  40.1 us
    all_to_all x7, waiting for transfers between devices, exchange(): return lax.all_to_all(pieces, axes, 0, 0, tiled=True)  18.3 us
    dot_general x8, matrix products, dot(): lax.dot_general(left, right, (dims, ((), ())), preferred_element_type=F32)  11.3 us
    ppermute x1, starting transfers between devices, step(): lax.ppermute(block, order, perm)  7.73 us
    dot_general x4, matrix products, batched(): return lax.dot_general(left, right, dims, preferred_element_type=F32)  7.46 us
    unnamed x45, local copies, waits for them, and re-layouts  6.45 us
  transfers between devices with their start and end apart: 38, of which 21 were waited for; matrix products, arithmetic and copies ran while one was open for 30% of the time, Pallas kernels for 0%

commit v1 on v0

--- a/solution.py
+++ b/solution.py
@@ -55,17 +55,19 @@
     return exchange(jnp.broadcast_to(value[None], (size,) + value.shape), axes)
 
 
-def gather_ring(value, z):
+def gather_line(value, z):
     tail = (0,) * value.ndim
-    canvas = place(jnp.zeros((8,) + value.shape, value.dtype), value[None], z, *tail)
-
-    def pass_on(k, carry):
-        up, down, canvas = carry
-        up, down = shift(up, "z", 8, 1), shift(down, "z", 8, -1)
-        canvas = place(canvas, up, (z - 1 - k) & 7, *tail)
-        return up, down, place(canvas, down, (z + 1 + k) & 7, *tail)
-
-    return lax.fori_loop(0, 4, pass_on, (value[None], value[None], canvas))[2]
+    inner = [(i, i ^ 1) for i in range(8)]
+    outer = [(i, (i + 1) & 7 if i & 1 else (i - 1) & 7) for i in range(8)]
+    pair, side = z // 2, 2 * (z & 1) - 1
+    other = lax.ppermute(value, "z", inner)
+    last = ordered(z & 1, value[None], other[None], 0)
+    canvas = jnp.zeros((4, 2) + value.shape, value.dtype)
+    canvas = place(canvas, last[None], pair, 0, *tail)
+    for perm, slot in ((outer, pair + side), (inner, pair - side), (outer, pair + 2)):
+        last = lax.ppermute(last, "z", perm)
+        canvas = place(canvas, last[None], slot & 3, 0, *tail)
+    return canvas.reshape((8,) + value.shape)
 
 
 def after(value, *others):
@@ -84,20 +86,23 @@
     part = ds // 32
     slot = fs // 4
 
-    pair = ordered(xh, tokens, swap(tokens, "xh"), 0)
-    all_tokens = gather_four(
-        pair,
-        "y",
-        y,
-        jnp.zeros((rows, d_in), BF16),
-        lambda canvas, piece, i: place(canvas, piece, i * (2 * own), 0),
-    )
-
     row0 = z * wide + (xl * 2 + c) * part
     mine = jnp.concatenate(
         [lax.dynamic_slice_in_dim(m, row0, part, 0) for m in (gate_small, up_small)], 0
     )
-    proj = gather(mine, ("y", "xh"), 8)
+    lanes = -(-fs // 128) * 128
+    more = 2 * part * lanes // d_in
+    mine = jnp.pad(mine, ((0, 0), (0, lanes - fs))).reshape(more, d_in)
+    mine = jnp.concatenate([tokens, mine], 0)[None]
+    both = gather_four(
+        ordered(xh, mine, swap(mine, "xh"), 0),
+        "y",
+        y,
+        jnp.zeros((8, own + more, d_in), BF16),
+        lambda canvas, piece, i: place(canvas, piece, i * 2, 0, 0),
+    )
+    all_tokens = both[:, :own].reshape(rows, d_in)
+    proj = both[:, own:].reshape(8, 2 * part, lanes)[:, :, :fs]
     proj = jnp.transpose(proj, (1, 0, 2)).reshape(2 * part, 8 * fs)
     wt = dot(width_hidden, proj, ((1,), (1,))).astype(BF16)
     wt = wt.reshape(2, 2, quarter, 2 * part)
@@ -110,7 +115,7 @@
         for g in (0, 1)
     ]
     wt = jnp.concatenate(blocks, 0)
-    wt_blocks = gather_ring(wt, z)
+    wt_blocks = gather(wt, "z", 8)
     wt = jnp.transpose(wt_blocks, (1, 0, 2)).reshape(2 * quarter, ds)
 
     narrow = dot(all_tokens, width_in, ((1,), (0,))).astype(BF16)
@@ -123,12 +128,11 @@
     keep, send = pick(xl, gh[:, 0], gh[:, 1]), pick(xl, gh[:, 1], gh[:, 0])
     gh = ordered(xl, keep[:, None], swap(send, "xl")[:, None], 1)
 
-    narrow_part = narrow
     narrow = gather(narrow, CHIPS, 16).reshape(2, 8, rows, wide)
     narrow = jnp.transpose(narrow, (0, 2, 1, 3)).reshape(2 * rows, ds)
     narrow = jnp.concatenate([narrow, swap(narrow, "c")], 0)
 
-    block = lax.dynamic_slice_in_dim(pick(c, after(gate_small, narrow_part), up_small), z * wide, wide, 0)
+    block = lax.dynamic_slice_in_dim(pick(c, gate_small, up_small), z * wide, wide, 0)
     block = pick(xl, block[:, : fs // 2], block[:, fs // 2 :])
     block = jnp.transpose(block.reshape(wide, 2, slot), (1, 2, 0))
     order = ("xl", "z", "c", "y", "xh")
@@ -162,7 +166,7 @@
     back = back.reshape(16, rows, wide)
     m_part = exchange(jnp.transpose(m_part, (1, 0, 2, 3)).astype(BF16), "z")
     m_own = jnp.sum(m_part.astype(F32), 0).astype(BF16)
-    m_all = gather_ring(m_own, z)
+    m_all = gather_line(m_own, z)
     m_all = jnp.transpose(m_all, (1, 0, 2, 3)).reshape(ds, 2 * quarter)
 
     d_narrow = jnp.sum(exchange(back, CHIPS).astype(F32), 0).astype(BF16)

time: 243 us -> 216 us (0.89)
  starting transfers between devices: 93.6 us -> 74.2 us
  local copies, waits for them, and re-layouts: 48.4 us -> 33.3 us
  waiting for transfers between devices: 70.8 us -> 78.4 us
    ppermute x30 -> x14, starting transfers between devices: 40.1 us -> 12.1 us  [shift(): lax.ppermute(value, axis, [(i, (i + step) % size) for i in range(size)])]
    ppermute x0 -> x4, waiting for transfers between devices: none -> 24.4 us  [the longest x3 22 us: gather_line(): last = lax.ppermute(last, 'z', perm)]
    ppermute x30 -> x14, waiting for transfers between devices: 52.5 us -> 40.8 us  [shift(): lax.ppermute(value, axis, [(i, (i + step) % size) for i in range(size)])]
    all_to_all x7, waiting for transfers between devices: 18.3 us -> 7.05 us  [exchange(): return lax.all_to_all(pieces, axes, 0, 0, tiled=True)]
    ppermute x1, waiting for transfers between devices: 0.01 us -> 6.16 us  [step(): lax.ppermute(block, order, perm)]
    dynamic_update_slice x20 -> x6, local copies, waits for them, and re-layouts: 5.42 us -> 1.13 us  [place(): return lax.dynamic_update_slice(canvas, piece, start)]
    ppermute x0 -> x4, starting transfers between devices: none -> 3.99 us  [the longest x3 3.12 us: gather_line(): last = lax.ppermute(last, 'z', perm)]
    all_to_all x7, starting transfers between devices: 45.7 us -> 49.5 us  [exchange(): return lax.all_to_all(pieces, axes, 0, 0, tiled=True)]
  transfers between devices with their start and end apart: 38 -> 26, of which waited for: 21 -> 14; matrix products, arithmetic and copies ran while one was open for 30% -> 23% of each run, Pallas kernels for 0% -> 0%
where the time goes in v1:
time: 216 us; the launch traced here: 214 us
  waiting for transfers between devices  78.4 us (36%)
  starting transfers between devices  74.2 us (34%)
  local copies, waits for them, and re-layouts  33.3 us (15%)
  matrix products  18.9 us (9%)
  other arithmetic  8.18 us (4%)
    all_to_all x7, starting transfers between devices, exchange(): return lax.all_to_all(pieces, axes, 0, 0, tiled=True)  49.5 us
    ppermute x14, waiting for transfers between devices, shift(): lax.ppermute(value, axis, [(i, (i + step) % size) for i in range(size)])  40.8 us
    ppermute x3, waiting for transfers between devices, gather_line(): last = lax.ppermute(last, 'z', perm)  22 us
    ppermute x14, starting transfers between devices, shift(): lax.ppermute(value, axis, [(i, (i + step) % size) for i in range(size)])  12.1 us
    dot_general x8, matrix products, dot(): lax.dot_general(left, right, (dims, ((), ())), preferred_element_type=F32)  10.3 us
    ppermute x1, starting transfers between devices, step(): lax.ppermute(block, order, perm)  8.69 us
    dot_general x4, matrix products, batched(): return lax.dot_general(left, right, dims, preferred_element_type=F32)  8.63 us
    all_to_all x7, waiting for transfers between devices, exchange(): return lax.all_to_all(pieces, axes, 0, 0, tiled=True)  7.05 us
  transfers between devices with their start and end apart: 26, of which 14 were waited for; matrix products, arithmetic and copies ran while one was open for 23% of the time, Pallas kernels for 0%

profile of v1, /device:TPU:8, one launch (start us, length us, event | category | flops | bytes accessed | tf_op | source)
XLA Modules:
  0.0 214.4 jit_solution(4773309915943215594)
XLA Ops:
  3.0 3.1 %collective-permute-start = (bf16[1,36,2048]{2,1,0:T(8,128)(2,1)S(1)}, bf16[1,36,2048]{2,1,0:T(8,128)(2,1)S(1)}, u32[]{:S(2)}, u32[]{:S(2)}) collective-permute-start(bf16[1,36,2048]{2,1,0:T(8,128)(2,1)S(1)} %maximum_bitcast_fusion), channel_id=1, source_target_pairs={{0,1},{1,0},{2,3},{3,2},{4,5},{5,4},{6,7},{7,6},{8,9},{9,8},{10,11... | collective-permute-start | bytes 442376 | tf_op jit(solution)/shard_map/ppermute | solution.py:17
  6.1 4.4 %collective-permute-done = bf16[1,36,2048]{2,1,0:T(8,128)(2,1)S(1)} collective-permute-done((bf16[1,36,2048]{2,1,0:T(8,128)(2,1)S(1)}, bf16[1,36,2048]{2,1,0:T(8,128)(2,1)S(1)}, u32[]{:S(2)}, u32[]{:S(2)}) %collective-permute-start) | collective-permute-done | bytes 147488 | tf_op jit(solution)/shard_map/ppermute | solution.py:17
  10.8 1.7 collective-permute-start.1
  12.9 2.3 %collective-permute-start.3 = (bf16[2,36,2048]{2,1,0:T(8,128)(2,1)S(1)}, bf16[2,36,2048]{2,1,0:T(8,128)(2,1)S(1)}, u32[]{:S(2)}, u32[]{:S(2)}) collective-permute-start(bf16[2,36,2048]{2,1,0:T(8,128)(2,1)S(1)} %get-tuple-element.7), channel_id=1, source_target_pairs={{0,4},{2,6},{4,0},{6,2},{1,5},{3,7},{5,1},{7,3},{8,12},{10,14},{12... | collective-permute-start | bytes 884744 | tf_op jit(solution)/shard_map/ppermute | solution.py:17
  15.2 6.3 %collective-permute-done.1 = bf16[2,36,2048]{2,1,0:T(8,128)(2,1)S(1)} collective-permute-done((bf16[2,36,2048]{2,1,0:T(8,128)(2,1)S(1)}, bf16[2,36,2048]{2,1,0:T(8,128)(2,1)S(1)}, u32[]{:S(2)}, u32[]{:S(2)}) %collective-permute-start.1) | collective-permute-done | bytes 294944 | tf_op jit(solution)/shard_map/ppermute | solution.py:17
  22.3 6.2 %collective-permute-done.3 = bf16[2,36,2048]{2,1,0:T(8,128)(2,1)S(1)} collective-permute-done((bf16[2,36,2048]{2,1,0:T(8,128)(2,1)S(1)}, bf16[2,36,2048]{2,1,0:T(8,128)(2,1)S(1)}, u32[]{:S(2)}, u32[]{:S(2)}) %collective-permute-start.3) | collective-permute-done | bytes 294944 | tf_op jit(solution)/shard_map/ppermute | solution.py:17
  29.7 3.3 %fusion.5 = bf16[688,64]{0,1:T(8,128)(2,1)S(1)} fusion(bf16[64,2752]{1,0:T(8,128)(2,1)S(1)} %reshape.278, bf16[688,2752]{1,0:T(8,128)(2,1)} %param.11), kind=kOutput, calls=%fused_computation.16 | convolution fusion | flops 242396160 | bytes 4227072 | tf_op jit(solution)/shard_map/dot_general | solution.py:13
  35.2 6.5 %all-to-all-start = ((bf16[16,192,128]{2,1,0:T(8,128)(2,1)}), bf16[16,192,128]{2,1,0:T(8,128)(2,1)S(1)}, u32[]{:S(2)}, u32[]{:S(2)}) async-start(bf16[16,192,128]{2,1,0:T(8,128)(2,1)} %broadcast_in_dim.43), calls=%async_computation | async-start | bytes 1572864 | tf_op jit(solution)/shard_map/all_to_all | solution.py:51
  41.9 1.6 collective-permute-start.8
  43.5 10.5 %collective-permute-done.8 = bf16[2,172,64]{1,2,0:T(8,128)(2,1)S(1)} collective-permute-done((bf16[2,172,64]{1,2,0:T(8,128)(2,1)S(1)}, bf16[2,172,64]{1,2,0:T(8,128)(2,1)S(1)}, u32[]{:S(2)}, u32[]{:S(2)}) %collective-permute-start.8) | collective-permute-done | bytes 44064 | tf_op jit(solution)/shard_map/ppermute | solution.py:17
  55.7 8.5 %all-to-all-start.1 = ((bf16[8,344,128]{2,1,0:T(8,128)(2,1)}), bf16[8,344,128]{2,1,0:T(8,128)(2,1)}, u32[]{:S(2)}, u32[]{:S(2)}) async-start(bf16[8,344,128]{2,1,0:T(8,128)(2,1)} %broadcast_in_dim.46), calls=%async_computation.1 | async-start | bytes 1409024 | tf_op jit(solution)/shard_map/all_to_all | solution.py:51
  68.2 8.7 %collective-permute-start.15 = (bf16[2,86,128]{2,1,0:T(8,128)(2,1)S(1)}, bf16[2,86,128]{2,1,0:T(8,128)(2,1)S(1)}, u32[]{:S(2)}, u32[]{:S(2)}) collective-permute-start(bf16[2,86,128]{2,1,0:T(8,128)(2,1)S(1)} %bitcast.221), channel_id=1, source_target_pairs={{0,0},{1,32},{2,64},{3,96},{4,128},{5,160},{6,192},{7,224},{8,8},{... | collective-permute-start | bytes 132104 | tf_op jit(solution)/shard_map/ppermute | solution.py:144
  76.9 6.2 %collective-permute-done.15 = bf16[2,86,128]{2,1,0:T(8,128)(2,1)S(1)} collective-permute-done((bf16[2,86,128]{2,1,0:T(8,128)(2,1)S(1)}, bf16[2,86,128]{2,1,0:T(8,128)(2,1)S(1)}, u32[]{:S(2)}, u32[]{:S(2)}) %collective-permute-start.15) | collective-permute-done | bytes 44064 | tf_op jit(solution)/shard_map/ppermute | solution.py:144
  85.5 1.2 broadcast_in_dim.103
  86.7 10.3 %all-to-all-start.6 = ((bf16[16,2,86,128]{3,1,2,0:T(2,128)(2,1)}), bf16[16,2,86,128]{3,1,2,0:T(2,128)(2,1)S(1)}, u32[]{:S(2)}, u32[]{:S(2)}) async-start(bf16[16,2,86,128]{3,1,2,0:T(2,128)(2,1)} %broadcast_in_dim.103), calls=%async_computation.6 | async-start | bytes 1409024 | tf_op jit(solution)/shard_map/all_to_all | solution.py:51
  97.0 1.2 fusion.35
  98.6 1.1 copy-done.4
  99.7 1.2 constant_dynamic-update-slice_fusion
  106.1 5.6 %all-to-all-start.4 = ((bf16[8,2,64,344]{3,2,1,0:T(8,128)(2,1)}), bf16[8,2,64,344]{3,2,1,0:T(8,128)(2,1)}, u32[]{:S(2)}, u32[]{:S(2)}) async-start(bf16[8,2,64,344]{3,2,1,0:T(8,128)(2,1)} %copy.171), calls=%async_computation.4 | async-start | bytes 1572864 | tf_op jit(solution)/shard_map/all_to_all | solution.py:51
  111.8 2.8 %convolution_convert_fusion.1 = bf16[8,384,128]{2,1,0:T(8,128)(2,1)} fusion(bf16[8,344,128]{2,1,0:T(8,128)(2,1)} %all-to-all-done.1, bf16[384,344]{0,1:T(8,128)(2,1)S(1)} %get-tuple-element.13), kind=kOutput, calls=%fused_computation.5 | convolution fusion | flops 270925824 | bytes 1755136 | tf_op jit(solution)/shard_map/dot_general | solution.py:22
  114.6 1.4 dynamic-slice_bitcast_fusion
  116.1 1.4 dot_general.48
  117.5 1.2 copy.241
  119.7 1.5 reshape.290
  121.2 1.4 copy.188
  123.1 2.2 %add_convert_fusion = bf16[8,384,128]{2,1,0:T(8,128)(2,1)S(1)} fusion(bf16[8,384,128]{2,1,0:T(8,128)(2,1)} %collective-permute-done.9, bf16[8,344,128]{2,1,0:T(8,128)(2,1)} %all-to-all-done.1, bf16[384,344]{0,1:T(8,128)(2,1)S(1)} %copy-done.10), kind=kOutput, calls=%fused_computation.2 | convolution fusion | flops 271712256 | bytes 2541568 | tf_op jit(solution)/shard_map/dot_general | solution.py:22
  126.3 6.5 %all-to-all-done.4 = bf16[8,2,64,344]{3,2,1,0:T(8,128)(2,1)} async-done(((bf16[8,2,64,344]{3,2,1,0:T(8,128)(2,1)}), bf16[8,2,64,344]{3,2,1,0:T(8,128)(2,1)}, u32[]{:S(2)}, u32[]{:S(2)}) %all-to-all-start.4) | async-done | bytes 704544 | tf_op jit(solution)/shard_map/all_to_all | solution.py:51
  132.8 6.6 %all-to-all-start.2 = ((bf16[16,192,128]{2,1,0:T(8,128)(2,1)}), bf16[16,192,128]{2,1,0:T(8,128)(2,1)}, u32[]{:S(2)}, u32[]{:S(2)}) async-start(bf16[16,192,128]{2,1,0:T(8,128)(2,1)} %bitcast.33), calls=%async_computation.2 | async-start | bytes 1572864 | tf_op jit(solution)/shard_map/all_to_all | solution.py:51
  139.5 1.3 reduce_sum.44
  141.7 1.4 fusion
  143.3 2.4 %collective-permute-done.11 = bf16[2,64,344]{2,1,0:T(8,128)(2,1)S(1)} collective-permute-done((bf16[2,64,344]{2,1,0:T(8,128)(2,1)S(1)}, bf16[2,64,344]{2,1,0:T(8,128)(2,1)S(1)}, u32[]{:S(2)}, u32[]{:S(2)}) %collective-permute-start.11) | collective-permute-done | bytes 88096 | tf_op jit(solution)/shard_map/ppermute | solution.py:63
  146.0 6.7 %collective-permute-done.12 = bf16[2,2,64,344]{3,2,1,0:T(8,128)(2,1)S(1)} collective-permute-done((bf16[2,2,64,344]{3,2,1,0:T(8,128)(2,1)S(1)}, bf16[2,2,64,344]{3,2,1,0:T(8,128)(2,1)S(1)}, u32[]{:S(2)}, u32[]{:S(2)}) %collective-permute-start.12) | collective-permute-done | bytes 176160 | tf_op jit(solution)/shard_map/ppermute | solution.py:68
  152.7 1.2 reduce_sum.42
  154.0 1.3 convolution_convert_fusion
  155.3 4.7 %all-to-all-start.3 = ((bf16[32,64,128]{2,1,0:T(8,128)(2,1)}), bf16[32,64,128]{2,1,0:T(8,128)(2,1)}, u32[]{:S(2)}, u32[]{:S(2)}) async-start(bf16[32,64,128]{2,1,0:T(8,128)(2,1)} %bitcast.199), calls=%async_computation.3 | async-start | bytes 1048576 | tf_op jit(solution)/shard_map/all_to_all | solution.py:51
  160.0 3.0 %collective-permute-start.14 = (bf16[2,2,64,344]{3,2,1,0:T(8,128)(2,1)}, bf16[2,2,64,344]{3,2,1,0:T(8,128)(2,1)S(1)}, u32[]{:S(2)}, u32[]{:S(2)}) collective-permute-start(bf16[2,2,64,344]{3,2,1,0:T(8,128)(2,1)} %collective-permute-done.13), channel_id=1, source_target_pairs={{0,112},{16,32},{32,16},{48,64},{64,48},{80,96},{96,80},{112,0},{1... | collective-permute-start | bytes 528392 | tf_op jit(solution)/shard_map/ppermute | solution.py:68
  164.0 15.4 %collective-permute-done.14 = bf16[2,2,64,344]{3,2,1,0:T(8,128)(2,1)S(1)} collective-permute-done((bf16[2,2,64,344]{3,2,1,0:T(8,128)(2,1)}, bf16[2,2,64,344]{3,2,1,0:T(8,128)(2,1)S(1)}, u32[]{:S(2)}, u32[]{:S(2)}) %collective-permute-start.14) | collective-permute-done | bytes 176160 | tf_op jit(solution)/shard_map/ppermute | solution.py:68
  179.4 1.2 fusion.34
  180.7 1.2 copy.190
  181.9 1.2 copy.184
  183.1 1.7 fusion.15
  184.8 1.9 fusion.4
  186.8 1.3 collective-permute-done.17
  188.2 1.7 add_convert_fusion.1
  191.3 7.2 %all-to-all-start.5 = ((bf16[16,64,344]{2,1,0:T(8,128)(2,1)}), bf16[16,64,344]{2,1,0:T(8,128)(2,1)S(1)}, u32[]{:S(2)}, u32[]{:S(2)}) async-start(bf16[16,64,344]{2,1,0:T(8,128)(2,1)} %bitcast.53), calls=%async_computation.5 | async-start | bytes 1572864 | tf_op jit(solution)/shard_map/all_to_all | solution.py:51
  198.5 1.6 collective-permute-start.18
  200.0 10.9 %collective-permute-done.18 = bf16[2,172,86]{2,1,0:T(8,128)(2,1)S(1)} collective-permute-done((bf16[2,172,86]{2,1,0:T(8,128)(2,1)S(1)}, bf16[2,172,86]{2,1,0:T(8,128)(2,1)S(1)}, u32[]{:S(2)}, u32[]{:S(2)}) %collective-permute-start.18) | collective-permute-done | bytes 59200 | tf_op jit(solution)/shard_map/ppermute | solution.py:17
  211.9 1.7 convert_reduce_fusion.1
  (131 shorter events, 29.1 us)
Async XLA Ops:
  0.6 32.9 %copy-start = (bf16[2048,128]{1,0:T(8,128)(2,1)S(1)}, bf16[2048,128]{1,0:T(8,128)(2,1)}, u32[]{:S(2)}) copy-start(bf16[2048,128]{1,0:T(8,128)(2,1)} %param.8) | copy-start | bytes 1572868
  3.0 7.5 %collective-permute-start = (bf16[1,36,2048]{2,1,0:T(8,128)(2,1)S(1)}, bf16[1,36,2048]{2,1,0:T(8,128)(2,1)S(1)}, u32[]{:S(2)}, u32[]{:S(2)}) collective-permute-start(bf16[1,36,2048]{2,1,0:T(8,128)(2,1)S(1)} %maximum_bitcast_fusion), channel_id=1, source_target_pairs={{0,1},{1,0},{2,3},{3,2},{4,5},{5,4},{6,7},{7,6},{8,9},{9,8},{10,11... | collective-permute-start | bytes 442376 | tf_op jit(solution)/shard_map/ppermute | solution.py:17
  10.8 10.7 %collective-permute-start.1 = (bf16[2,36,2048]{2,1,0:T(8,128)(2,1)S(1)}, bf16[2,36,2048]{2,1,0:T(8,128)(2,1)S(1)}, u32[]{:S(2)}, u32[]{:S(2)}) collective-permute-start(bf16[2,36,2048]{2,1,0:T(8,128)(2,1)S(1)} %get-tuple-element.7), channel_id=1, source_target_pairs={{0,2},{2,4},{4,6},{6,0},{1,3},{3,5},{5,7},{7,1},{8,10},{10,12},{12... | collective-permute-start | bytes 884744 | tf_op jit(solution)/shard_map/ppermute | solution.py:17
  12.4 9.9 %collective-permute-start.2 = (bf16[2,36,2048]{2,1,0:T(8,128)(2,1)S(1)}, bf16[2,36,2048]{2,1,0:T(8,128)(2,1)S(1)}, u32[]{:S(2)}, u32[]{:S(2)}) collective-permute-start(bf16[2,36,2048]{2,1,0:T(8,128)(2,1)S(1)} %get-tuple-element.7), channel_id=1, source_target_pairs={{0,6},{2,0},{4,2},{6,4},{1,7},{3,1},{5,3},{7,5},{8,14},{10,8},{12,... | collective-permute-start | bytes 884744 | tf_op jit(solution)/shard_map/ppermute | solution.py:17
  12.9 15.6 %collective-permute-start.3 = (bf16[2,36,2048]{2,1,0:T(8,128)(2,1)S(1)}, bf16[2,36,2048]{2,1,0:T(8,128)(2,1)S(1)}, u32[]{:S(2)}, u32[]{:S(2)}) collective-permute-start(bf16[2,36,2048]{2,1,0:T(8,128)(2,1)S(1)} %get-tuple-element.7), channel_id=1, source_target_pairs={{0,4},{2,6},{4,0},{6,2},{1,5},{3,7},{5,1},{7,3},{8,12},{10,14},{12... | collective-permute-start | bytes 884744 | tf_op jit(solution)/shard_map/ppermute | solution.py:17
  33.0 1.0 copy-start.5
  33.4 8.4 %collective-permute-start.7 = (bf16[2,172,64]{1,2,0:T(8,128)(2,1)S(1)}, bf16[2,172,64]{1,2,0:T(8,128)(2,1)S(1)}, u32[]{:S(2)}, u32[]{:S(2)}) collective-permute-start(bf16[2,172,64]{1,2,0:T(8,128)(2,1)S(1)} %get-tuple-element.23), channel_id=1, source_target_pairs={{0,8},{8,0},{1,9},{9,1},{2,10},{10,2},{3,11},{11,3},{4,12},{12,4},... | collective-permute-start | bytes 132104 | tf_op jit(solution)/shard_map/ppermute | solution.py:17
  35.2 19.5 %all-to-all-start = ((bf16[16,192,128]{2,1,0:T(8,128)(2,1)}), bf16[16,192,128]{2,1,0:T(8,128)(2,1)S(1)}, u32[]{:S(2)}, u32[]{:S(2)}) async-start(bf16[16,192,128]{2,1,0:T(8,128)(2,1)} %broadcast_in_dim.43), calls=%async_computation | async-start | bytes 1572864 | tf_op jit(solution)/shard_map/all_to_all | solution.py:51
  41.9 12.1 %collective-permute-start.8 = (bf16[2,172,64]{1,2,0:T(8,128)(2,1)S(1)}, bf16[2,172,64]{1,2,0:T(8,128)(2,1)S(1)}, u32[]{:S(2)}, u32[]{:S(2)}) collective-permute-start(bf16[2,172,64]{1,2,0:T(8,128)(2,1)S(1)} %get-tuple-element.33), channel_id=1, source_target_pairs={{0,128},{128,0},{1,129},{129,1},{2,130},{130,2},{3,131},{131,3},{4... | collective-permute-start | bytes 132104 | tf_op jit(solution)/shard_map/ppermute | solution.py:17
  55.7 29.8 %all-to-all-start.1 = ((bf16[8,344,128]{2,1,0:T(8,128)(2,1)}), bf16[8,344,128]{2,1,0:T(8,128)(2,1)}, u32[]{:S(2)}, u32[]{:S(2)}) async-start(bf16[8,344,128]{2,1,0:T(8,128)(2,1)} %broadcast_in_dim.46), calls=%async_computation.1 | async-start | bytes 1409024 | tf_op jit(solution)/shard_map/all_to_all | solution.py:51
  64.3 1.5 collective-permute-start.4
  65.9 17.2 %collective-permute-start.5 = (bf16[2,192,172]{1,2,0:T(8,128)(2,1)S(1)}, bf16[2,192,172]{1,2,0:T(8,128)(2,1)S(1)}, u32[]{:S(2)}, u32[]{:S(2)}) collective-permute-start(bf16[2,192,172]{1,2,0:T(8,128)(2,1)S(1)} %get-tuple-element.15), channel_id=1, source_target_pairs={{0,128},{128,0},{1,129},{129,1},{2,130},{130,2},{3,131},{131,3},{4... | collective-permute-start | bytes 396296 | tf_op jit(solution)/shard_map/ppermute | solution.py:17
  68.1 30.5 %collective-permute-start.6 = (bf16[384,1024]{1,0:T(8,128)(2,1)}, bf16[384,1024]{1,0:T(8,128)(2,1)}, u32[]{:S(2)}, u32[]{:S(2)}) collective-permute-start(bf16[384,1024]{1,0:T(8,128)(2,1)} %bitcast.188), channel_id=1, source_target_pairs={{0,8},{8,0},{1,9},{9,1},{2,10},{10,2},{3,11},{11,3},{4,12},{12,4},... | collective-permute-start | bytes 2359304 | tf_op jit(solution)/shard_map/ppermute | solution.py:17
  68.2 14.8 %collective-permute-start.15 = (bf16[2,86,128]{2,1,0:T(8,128)(2,1)S(1)}, bf16[2,86,128]{2,1,0:T(8,128)(2,1)S(1)}, u32[]{:S(2)}, u32[]{:S(2)}) collective-permute-start(bf16[2,86,128]{2,1,0:T(8,128)(2,1)S(1)} %bitcast.221), channel_id=1, source_target_pairs={{0,0},{1,32},{2,64},{3,96},{4,128},{5,160},{6,192},{7,224},{8,8},{... | collective-permute-start | bytes 132104 | tf_op jit(solution)/shard_map/ppermute | solution.py:144
  86.7 19.4 %all-to-all-start.6 = ((bf16[16,2,86,128]{3,1,2,0:T(2,128)(2,1)}), bf16[16,2,86,128]{3,1,2,0:T(2,128)(2,1)S(1)}, u32[]{:S(2)}, u32[]{:S(2)}) async-start(bf16[16,2,86,128]{3,1,2,0:T(2,128)(2,1)} %broadcast_in_dim.103), calls=%async_computation.6 | async-start | bytes 1409024 | tf_op jit(solution)/shard_map/all_to_all | solution.py:51
  98.3 1.4 copy-start.4
  101.7 0.7 copy-start.6
  102.4 0.7 copy-start.8
  104.2 1.0 copy-start.7
  104.2 1.1 copy-start.9
  106.1 8.5 %copy-start.3 = (bf16[16,2,86,128]{3,1,2,0:T(2,128)(2,1)}, bf16[16,2,86,128]{3,1,2,0:T(2,128)(2,1)S(1)}, u32[]{:S(2)}) copy-start(bf16[16,2,86,128]{3,1,2,0:T(2,128)(2,1)S(1)} %all-to-all-done.6) | copy-start | bytes 2113540
  106.1 26.7 %all-to-all-start.4 = ((bf16[8,2,64,344]{3,2,1,0:T(8,128)(2,1)}), bf16[8,2,64,344]{3,2,1,0:T(8,128)(2,1)}, u32[]{:S(2)}, u32[]{:S(2)}) async-start(bf16[8,2,64,344]{3,2,1,0:T(8,128)(2,1)} %copy.171), calls=%async_computation.4 | async-start | bytes 1572864 | tf_op jit(solution)/shard_map/all_to_all | solution.py:51
  114.6 8.5 %collective-permute-start.9 = (bf16[8,384,128]{2,1,0:T(8,128)(2,1)}, bf16[8,384,128]{2,1,0:T(8,128)(2,1)}, u32[]{:S(2)}, u32[]{:S(2)}) collective-permute-start(bf16[8,384,128]{2,1,0:T(8,128)(2,1)} %convolution_convert_fusion.1), channel_id=1, source_target_pairs={{0,8},{8,0},{1,9},{9,1},{2,10},{10,2},{3,11},{11,3},{4,12},{12,4},... | collective-permute-start | bytes 2359304 | tf_op jit(solution)/shard_map/ppermute | solution.py:17
  119.7 3.5 %copy-start.10 = (bf16[384,344]{0,1:T(8,128)(2,1)S(1)}, bf16[384,344]{0,1:T(8,128)(2,1)}, u32[]{:S(2)}) copy-start(bf16[384,344]{0,1:T(8,128)(2,1)} %get-tuple-element.12) | copy-start | bytes 792580
  121.2 4.2 %copy-start.1 = (bf16[4,86,1024]{2,1,0:T(8,128)(2,1)}, bf16[4,86,1024]{2,1,0:T(8,128)(2,1)S(1)}, u32[]{:S(2)}) copy-start(bf16[4,86,1024]{2,1,0:T(8,128)(2,1)S(1)} %reshape.290) | copy-start | bytes 2113540
  122.6 60.5 %collective-permute-start.16 = (bf16[4,86,1024]{2,0,1:T(4,128)(2,1)}, bf16[4,86,1024]{2,0,1:T(4,128)(2,1)}, u32[]{:S(2)}, u32[]{:S(2)}) collective-permute-start(bf16[4,86,1024]{2,0,1:T(4,128)(2,1)} %copy.188), channel_id=1, source_target_pairs={{0,8},{8,0},{1,9},{9,1},{2,10},{10,2},{3,11},{11,3},{4,12},{12,4},... | collective-permute-start | bytes 2113544 | tf_op jit(solution)/shard_map/ppermute | solution.py:17
  132.8 19.9 %all-to-all-start.2 = ((bf16[16,192,128]{2,1,0:T(8,128)(2,1)}), bf16[16,192,128]{2,1,0:T(8,128)(2,1)}, u32[]{:S(2)}, u32[]{:S(2)}) async-start(bf16[16,192,128]{2,1,0:T(8,128)(2,1)} %bitcast.33), calls=%async_computation.2 | async-start | bytes 1572864 | tf_op jit(solution)/shard_map/all_to_all | solution.py:51
  140.7 4.9 %collective-permute-start.11 = (bf16[2,64,344]{2,1,0:T(8,128)(2,1)S(1)}, bf16[2,64,344]{2,1,0:T(8,128)(2,1)S(1)}, u32[]{:S(2)}, u32[]{:S(2)}) collective-permute-start(bf16[2,64,344]{2,1,0:T(8,128)(2,1)S(1)} %reduce_sum.44), channel_id=1, source_target_pairs={{0,16},{16,0},{32,48},{48,32},{64,80},{80,64},{96,112},{112,96},{1... | collective-permute-start | bytes 264200 | tf_op jit(solution)/shard_map/ppermute | solution.py:63
  143.2 45.0 %collective-permute-start.10 = (bf16[8,128,344]{1,2,0:T(8,128)(2,1)}, bf16[8,128,344]{1,2,0:T(8,128)(2,1)}, u32[]{:S(2)}, u32[]{:S(2)}) collective-permute-start(bf16[8,128,344]{1,2,0:T(8,128)(2,1)} %fusion), channel_id=1, source_target_pairs={{0,8},{8,0},{1,9},{9,1},{2,10},{10,2},{3,11},{11,3},{4,12},{12,4},... | collective-permute-start | bytes 2113544 | tf_op jit(solution)/shard_map/ppermute | solution.py:17
  145.7 7.0 %collective-permute-start.12 = (bf16[2,2,64,344]{3,2,1,0:T(8,128)(2,1)S(1)}, bf16[2,2,64,344]{3,2,1,0:T(8,128)(2,1)S(1)}, u32[]{:S(2)}, u32[]{:S(2)}) collective-permute-start(bf16[2,2,64,344]{3,2,1,0:T(8,128)(2,1)S(1)} %maximum_select_fusion.3), channel_id=1, source_target_pairs={{0,112},{16,32},{32,16},{48,64},{64,48},{80,96},{96,80},{112,0},{1... | collective-permute-start | bytes 528392 | tf_op jit(solution)/shard_map/ppermute | solution.py:68
  152.7 7.3 %collective-permute-start.13 = (bf16[2,2,64,344]{3,2,1,0:T(8,128)(2,1)S(1)}, bf16[2,2,64,344]{3,2,1,0:T(8,128)(2,1)}, u32[]{:S(2)}, u32[]{:S(2)}) collective-permute-start(bf16[2,2,64,344]{3,2,1,0:T(8,128)(2,1)S(1)} %collective-permute-done.12), channel_id=1, source_target_pairs={{0,16},{16,0},{32,48},{48,32},{64,80},{80,64},{96,112},{112,96},{1... | collective-permute-start | bytes 528392 | tf_op jit(solution)/shard_map/ppermute | solution.py:68
  155.3 36.0 %all-to-all-start.3 = ((bf16[32,64,128]{2,1,0:T(8,128)(2,1)}), bf16[32,64,128]{2,1,0:T(8,128)(2,1)}, u32[]{:S(2)}, u32[]{:S(2)}) async-start(bf16[32,64,128]{2,1,0:T(8,128)(2,1)} %bitcast.199), calls=%async_computation.3 | async-start | bytes 1048576 | tf_op jit(solution)/shard_map/all_to_all | solution.py:51
  160.0 19.4 %collective-permute-start.14 = (bf16[2,2,64,344]{3,2,1,0:T(8,128)(2,1)}, bf16[2,2,64,344]{3,2,1,0:T(8,128)(2,1)S(1)}, u32[]{:S(2)}, u32[]{:S(2)}) collective-permute-start(bf16[2,2,64,344]{3,2,1,0:T(8,128)(2,1)} %collective-permute-done.13), channel_id=1, source_target_pairs={{0,112},{16,32},{32,16},{48,64},{64,48},{80,96},{96,80},{112,0},{1... | collective-permute-start | bytes 528392 | tf_op jit(solution)/shard_map/ppermute | solution.py:68
  179.4 3.7 %copy-start.2 = (bf16[4,86,1024]{2,1,0:T(8,128)(2,1)S(1)}, bf16[4,86,1024]{2,1,0:T(8,128)(2,1)}, u32[]{:S(2)}) copy-start(bf16[4,86,1024]{2,1,0:T(8,128)(2,1)} %copy-done.1) | copy-start | bytes 2113540
  186.7 1.4 collective-permute-start.17
  191.3 22.4 %all-to-all-start.5 = ((bf16[16,64,344]{2,1,0:T(8,128)(2,1)}), bf16[16,64,344]{2,1,0:T(8,128)(2,1)S(1)}, u32[]{:S(2)}, u32[]{:S(2)}) async-start(bf16[16,64,344]{2,1,0:T(8,128)(2,1)} %bitcast.53), calls=%async_computation.5 | async-start | bytes 1572864 | tf_op jit(solution)/shard_map/all_to_all | solution.py:51
  198.5 12.5 %collective-permute-start.18 = (bf16[2,172,86]{2,1,0:T(8,128)(2,1)S(1)}, bf16[2,172,86]{2,1,0:T(8,128)(2,1)S(1)}, u32[]{:S(2)}, u32[]{:S(2)}) collective-permute-start(bf16[2,172,86]{2,1,0:T(8,128)(2,1)S(1)} %fusion.30), channel_id=1, source_target_pairs={{0,128},{128,0},{1,129},{129,1},{2,130},{130,2},{3,131},{131,3},{4... | collective-permute-start | bytes 177512 | tf_op jit(solution)/shard_map/ppermute | solution.py:17

commit v2 on v1

--- a/solution.py
+++ b/solution.py
@@ -141,8 +141,13 @@
         sxl, sz, sc, sy, sxh = i // 128, i // 16 % 8, i // 8 % 2, i // 2 % 4, i % 2
         dz = (sy % 2) * 4 + sxh * 2 + sxl
         perm.append((i, (((sy // 2) * 8 + dz) * 2 + sc) * 8 + sz))
-    cols = gather(lax.ppermute(block, order, perm), CHIPS, 16).reshape(2, 8, 2, slot, wide)
-    cols = jnp.transpose(cols, (0, 2, 3, 1, 4)).reshape(4, slot, ds)
+    cols = lax.ppermute(block, order, perm)[None]
+    cols = ordered(xl, cols, swap(cols, "xl"), 0)
+    cols = ordered(xh, cols, swap(cols, "xh"), 3)
+    cols = ordered(y & 1, cols, lax.ppermute(cols, "y", [(0, 1), (1, 0), (2, 3), (3, 2)]), 3)
+    other = lax.ppermute(cols, "y", [(1, 2), (2, 1), (3, 0), (0, 3)])
+    cols = ordered(y // 2, cols, other, 3)
+    cols = cols.reshape(4, slot, ds)
     other = swap(cols, "c")
     cols_g, cols_u = pick(c, cols, other), pick(c, other, cols)
 

time: 216 us -> 221 us (1.023)
  waiting for transfers between devices: 78.4 us -> 93 us
  starting transfers between devices: 74.2 us -> 67.8 us
  local copies, waits for them, and re-layouts: 33.3 us -> 27 us
  other arithmetic: 8.18 us -> 12.6 us
    all_to_all x7 -> x6, waiting for transfers between devices: 7.05 us -> 20.2 us  [exchange(): return lax.all_to_all(pieces, axes, 0, 0, tiled=True)]
    all_to_all x7 -> x6, starting transfers between devices: 49.5 us -> 37.1 us  [exchange(): return lax.all_to_all(pieces, axes, 0, 0, tiled=True)]
    ppermute x14 -> x16, waiting for transfers between devices: 40.8 us -> 46.8 us  [shift(): lax.ppermute(value, axis, [(i, (i + step) % size) for i in range(size)])]
    ppermute x1 -> x3, waiting for transfers between devices: 6.16 us -> 0.62 us  [the longest x1 0.62 us: step(): cols = lax.ppermute(block, order, perm)[None]]
    select_n x15 -> x22, other arithmetic: 1.43 us -> 6.77 us  [pick(): return jnp.where(index == 0, first, second)]
    ppermute x14 -> x16, starting transfers between devices: 12.1 us -> 15.7 us  [shift(): lax.ppermute(value, axis, [(i, (i + step) % size) for i in range(size)])]
    reshape x2 -> x0, local copies, waits for them, and re-layouts: 2.93 us -> none  [step(): cols = jnp.transpose(cols, (0, 2, 3, 1, 4)).reshape(4, slot, ds)]
    ppermute x1 -> x3, starting transfers between devices: 8.69 us -> 11 us  [the longest x1 8.98 us: step(): cols = lax.ppermute(block, order, perm)[None]]
  transfers between devices with their start and end apart: 26 -> 29, of which waited for: 14 -> 17; matrix products, arithmetic and copies ran while one was open for 23% -> 25% of each run, Pallas kernels for 0% -> 0%
where the time goes in v2:
time: 221 us; the launch traced here: 220 us
  waiting for transfers between devices  93 us (42%)
  starting transfers between devices  67.8 us (31%)
  local copies, waits for them, and re-layouts  27 us (12%)
  matrix products  17.9 us (8%)
  other arithmetic  12.6 us (6%)
    ppermute x16, waiting for transfers between devices, shift(): lax.ppermute(value, axis, [(i, (i + step) % size) for i in range(size)])  46.8 us
    all_to_all x6, starting transfers between devices, exchange(): return lax.all_to_all(pieces, axes, 0, 0, tiled=True)  37.1 us
    ppermute x3, waiting for transfers between devices, gather_line(): last = lax.ppermute(last, 'z', perm)  23.1 us
    all_to_all x6, waiting for transfers between devices, exchange(): return lax.all_to_all(pieces, axes, 0, 0, tiled=True)  20.2 us
    ppermute x16, starting transfers between devices, shift(): lax.ppermute(value, axis, [(i, (i + step) % size) for i in range(size)])  15.7 us
    dot_general x8, matrix products, dot(): lax.dot_general(left, right, (dims, ((), ())), preferred_element_type=F32)  10.3 us
    ppermute x1, starting transfers between devices, step(): cols = lax.ppermute(block, order, perm)[None]  8.98 us
    dot_general x4, matrix products, batched(): return lax.dot_general(left, right, dims, preferred_element_type=F32)  7.59 us
  transfers between devices with their start and end apart: 29, of which 17 were waited for; matrix products, arithmetic and copies ran while one was open for 25% of the time, Pallas kernels for 0%

profile of v2, /device:TPU:8, one launch (start us, length us, event | category | flops | bytes accessed | tf_op | source)
XLA Modules:
  0.0 219.8 jit_solution(3051735953044552422)
XLA Ops:
  1.8 9.0 %collective-permute-start.15 = (bf16[2,86,128]{2,1,0:T(8,128)(2,1)S(1)}, bf16[2,86,128]{2,1,0:T(8,128)(2,1)S(1)}, u32[]{:S(2)}, u32[]{:S(2)}) collective-permute-start(bf16[2,86,128]{2,1,0:T(8,128)(2,1)S(1)} %bitcast.227), channel_id=1, source_target_pairs={{0,0},{1,32},{2,64},{3,96},{4,128},{5,160},{6,192},{7,224},{8,8},{... | collective-permute-start | bytes 132104 | tf_op jit(solution)/shard_map/ppermute | solution.py:144
  13.8 2.7 %collective-permute-done.16 = bf16[1,2,86,128]{3,2,1,0:T(8,128)(2,1)S(1)} collective-permute-done((bf16[1,2,86,128]{3,2,1,0:T(8,128)(2,1)S(1)}, bf16[1,2,86,128]{3,2,1,0:T(8,128)(2,1)S(1)}, u32[]{:S(2)}, u32[]{:S(2)}) %collective-permute-start.16) | collective-permute-done | bytes 44064 | tf_op jit(solution)/shard_map/ppermute | solution.py:17
  16.5 3.6 %collective-permute-start.17 = (bf16[2,2,86,128]{3,2,1,0:T(8,128)(2,1)S(1)}, bf16[2,2,86,128]{3,2,1,0:T(8,128)(2,1)S(1)}, u32[]{:S(2)}, u32[]{:S(2)}) collective-permute-start(bf16[2,2,86,128]{3,2,1,0:T(8,128)(2,1)S(1)} %maximum_select_fusion.13), channel_id=1, source_target_pairs={{0,1},{1,0},{2,3},{3,2},{4,5},{5,4},{6,7},{7,6},{8,9},{9,8},{10,11... | collective-permute-start | bytes 264200 | tf_op jit(solution)/shard_map/ppermute | solution.py:17
  20.2 3.3 %collective-permute-done.17 = bf16[2,2,86,128]{3,2,1,0:T(8,128)(2,1)S(1)} collective-permute-done((bf16[2,2,86,128]{3,2,1,0:T(8,128)(2,1)S(1)}, bf16[2,2,86,128]{3,2,1,0:T(8,128)(2,1)S(1)}, u32[]{:S(2)}, u32[]{:S(2)}) %collective-permute-start.17) | collective-permute-done | bytes 88096 | tf_op jit(solution)/shard_map/ppermute | solution.py:17
  23.7 3.3 %collective-permute-done = bf16[1,36,2048]{2,1,0:T(8,128)(2,1)S(1)} collective-permute-done((bf16[1,36,2048]{2,1,0:T(8,128)(2,1)S(1)}, bf16[1,36,2048]{2,1,0:T(8,128)(2,1)S(1)}, u32[]{:S(2)}, u32[]{:S(2)}) %collective-permute-start) | collective-permute-done | bytes 147488 | tf_op jit(solution)/shard_map/ppermute | solution.py:17
  27.3 4.5 %collective-permute-start.1 = (bf16[2,36,2048]{2,1,0:T(8,128)(2,1)S(1)}, bf16[2,36,2048]{2,1,0:T(8,128)(2,1)S(1)}, u32[]{:S(2)}, u32[]{:S(2)}) collective-permute-start(bf16[2,36,2048]{2,1,0:T(8,128)(2,1)S(1)} %get-tuple-element.7), channel_id=1, source_target_pairs={{0,2},{2,4},{4,6},{6,0},{1,3},{3,5},{5,7},{7,1},{8,10},{10,12},{12... | collective-permute-start | bytes 884744 | tf_op jit(solution)/shard_map/ppermute | solution.py:17
  31.9 1.7 collective-permute-start.3
  34.4 2.0 collective-permute-start.19
  36.4 10.2 %collective-permute-done.1 = bf16[2,36,2048]{2,1,0:T(8,128)(2,1)S(1)} collective-permute-done((bf16[2,36,2048]{2,1,0:T(8,128)(2,1)S(1)}, bf16[2,36,2048]{2,1,0:T(8,128)(2,1)S(1)}, u32[]{:S(2)}, u32[]{:S(2)}) %collective-permute-start.1) | collective-permute-done | bytes 294944 | tf_op jit(solution)/shard_map/ppermute | solution.py:17
  46.7 2.3 %collective-permute-done.2 = bf16[2,36,2048]{2,1,0:T(8,128)(2,1)S(1)} collective-permute-done((bf16[2,36,2048]{2,1,0:T(8,128)(2,1)S(1)}, bf16[2,36,2048]{2,1,0:T(8,128)(2,1)S(1)}, u32[]{:S(2)}, u32[]{:S(2)}) %collective-permute-start.2) | collective-permute-done | bytes 294944 | tf_op jit(solution)/shard_map/ppermute | solution.py:17
  50.2 3.3 %fusion.5 = bf16[688,64]{0,1:T(8,128)(2,1)S(1)} fusion(bf16[64,2752]{1,0:T(8,128)(2,1)S(1)} %reshape.288, bf16[688,2752]{1,0:T(8,128)(2,1)} %param.11), kind=kOutput, calls=%fused_computation.16 | convolution fusion | flops 242396160 | bytes 4227072 | tf_op jit(solution)/shard_map/dot_general | solution.py:13
  55.8 3.8 %all-to-all-start = ((bf16[16,192,128]{2,1,0:T(8,128)(2,1)}), bf16[16,192,128]{2,1,0:T(8,128)(2,1)S(1)}, u32[]{:S(2)}, u32[]{:S(2)}) async-start(bf16[16,192,128]{2,1,0:T(8,128)(2,1)} %broadcast_in_dim.43), calls=%async_computation | async-start | bytes 1572864 | tf_op jit(solution)/shard_map/all_to_all | solution.py:51
  59.7 1.6 collective-permute-start.8
  61.3 10.5 %collective-permute-done.8 = bf16[2,172,64]{1,2,0:T(8,128)(2,1)S(1)} collective-permute-done((bf16[2,172,64]{1,2,0:T(8,128)(2,1)S(1)}, bf16[2,172,64]{1,2,0:T(8,128)(2,1)S(1)}, u32[]{:S(2)}, u32[]{:S(2)}) %collective-permute-start.8) | collective-permute-done | bytes 44064 | tf_op jit(solution)/shard_map/ppermute | solution.py:17
  73.5 9.6 %all-to-all-start.1 = ((bf16[8,344,128]{2,1,0:T(8,128)(2,1)}), bf16[8,344,128]{2,1,0:T(8,128)(2,1)}, u32[]{:S(2)}, u32[]{:S(2)}) async-start(bf16[8,344,128]{2,1,0:T(8,128)(2,1)} %broadcast_in_dim.90), calls=%async_computation.1 | async-start | bytes 1409024 | tf_op jit(solution)/shard_map/all_to_all | solution.py:51
  85.7 1.2 copy.145
  88.5 1.4 maximum_select_fusion
  90.4 1.3 collective-permute-done.5
  94.2 9.3 %all-to-all-done.1 = bf16[8,344,128]{2,1,0:T(8,128)(2,1)} async-done(((bf16[8,344,128]{2,1,0:T(8,128)(2,1)}), bf16[8,344,128]{2,1,0:T(8,128)(2,1)}, u32[]{:S(2)}, u32[]{:S(2)}) %all-to-all-start.1) | async-done | bytes 704544 | tf_op jit(solution)/shard_map/all_to_all | solution.py:51
  103.5 1.2 fusion.31
  105.1 1.1 copy-done.2
  106.3 1.2 constant_dynamic-update-slice_fusion
  111.8 4.2 %all-to-all-start.4 = ((bf16[8,2,64,344]{3,2,1,0:T(8,128)(2,1)}), bf16[8,2,64,344]{3,2,1,0:T(8,128)(2,1)}, u32[]{:S(2)}, u32[]{:S(2)}) async-start(bf16[8,2,64,344]{3,2,1,0:T(8,128)(2,1)} %copy.125), calls=%async_computation.4 | async-start | bytes 1572864 | tf_op jit(solution)/shard_map/all_to_all | solution.py:51
  116.0 2.9 %convolution_convert_fusion.1 = bf16[8,384,128]{2,1,0:T(8,128)(2,1)} fusion(bf16[8,344,128]{2,1,0:T(8,128)(2,1)} %all-to-all-done.1, bf16[384,344]{0,1:T(8,128)(2,1)S(1)} %get-tuple-element.15), kind=kOutput, calls=%fused_computation.5 | convolution fusion | flops 270925824 | bytes 1755136 | tf_op jit(solution)/shard_map/dot_general | solution.py:22
  118.9 1.4 dynamic-slice_bitcast_fusion
  120.3 1.4 dot_general.48
  121.7 2.5 %broadcast_select_fusion.1 = (bf16[8,43,1024]{2,0,1:T(8,128)(2,1)}, bf16[8,43,1024]{2,0,1:T(8,128)(2,1)}) fusion(bf16[8,43,1024]{2,0,1:T(8,128)(2,1)} %bitcast.188, bf16[8,43,1024]{2,0,1:T(8,128)(2,1)} %bitcast.189, pred[]{:T(512)S(6)} %eq.14), kind=kLoop, calls=%fused_computation.33 | loop fusion | flops 704512 | bytes 2818049 | tf_op jit(solution)/shard_map/jit(_where)/select_n | solution.py:30
  124.3 2.2 %add_convert_fusion = bf16[8,384,128]{2,1,0:T(8,128)(2,1)S(1)} fusion(bf16[8,384,128]{2,1,0:T(8,128)(2,1)} %collective-permute-done.9, bf16[8,344,128]{2,1,0:T(8,128)(2,1)} %all-to-all-done.1, bf16[384,344]{0,1:T(8,128)(2,1)S(1)} %copy-done.4), kind=kOutput, calls=%fused_computation.2 | convolution fusion | flops 271712256 | bytes 2541568 | tf_op jit(solution)/shard_map/dot_general | solution.py:22
  127.5 10.4 %all-to-all-done.4 = bf16[8,2,64,344]{3,2,1,0:T(8,128)(2,1)} async-done(((bf16[8,2,64,344]{3,2,1,0:T(8,128)(2,1)}), bf16[8,2,64,344]{3,2,1,0:T(8,128)(2,1)}, u32[]{:S(2)}, u32[]{:S(2)}) %all-to-all-start.4) | async-done | bytes 704544 | tf_op jit(solution)/shard_map/all_to_all | solution.py:51
  137.8 7.5 %all-to-all-start.2 = ((bf16[16,192,128]{2,1,0:T(8,128)(2,1)}), bf16[16,192,128]{2,1,0:T(8,128)(2,1)}, u32[]{:S(2)}, u32[]{:S(2)}) async-start(bf16[16,192,128]{2,1,0:T(8,128)(2,1)} %bitcast.33), calls=%async_computation.2 | async-start | bytes 1572864 | tf_op jit(solution)/shard_map/all_to_all | solution.py:51
  145.3 1.3 reduce_sum.44
  147.6 1.5 fusion
  149.1 2.3 %collective-permute-done.11 = bf16[2,64,344]{2,1,0:T(8,128)(2,1)S(1)} collective-permute-done((bf16[2,64,344]{2,1,0:T(8,128)(2,1)S(1)}, bf16[2,64,344]{2,1,0:T(8,128)(2,1)S(1)}, u32[]{:S(2)}, u32[]{:S(2)}) %collective-permute-start.11) | collective-permute-done | bytes 88096 | tf_op jit(solution)/shard_map/ppermute | solution.py:63
  151.9 6.8 %collective-permute-done.12 = bf16[2,2,64,344]{3,2,1,0:T(8,128)(2,1)} collective-permute-done((bf16[2,2,64,344]{3,2,1,0:T(8,128)(2,1)S(1)}, bf16[2,2,64,344]{3,2,1,0:T(8,128)(2,1)}, u32[]{:S(2)}, u32[]{:S(2)}) %collective-permute-start.12) | collective-permute-done | bytes 176160 | tf_op jit(solution)/shard_map/ppermute | solution.py:68
  159.6 1.2 reduce_sum.42
  160.9 1.3 convolution_convert_fusion
  162.2 4.7 %all-to-all-start.3 = ((bf16[32,64,128]{2,1,0:T(8,128)(2,1)}), bf16[32,64,128]{2,1,0:T(8,128)(2,1)}, u32[]{:S(2)}, u32[]{:S(2)}) async-start(bf16[32,64,128]{2,1,0:T(8,128)(2,1)} %bitcast.200), calls=%async_computation.3 | async-start | bytes 1048576 | tf_op jit(solution)/shard_map/all_to_all | solution.py:51
  166.9 3.0 %collective-permute-start.14 = (bf16[2,2,64,344]{3,2,1,0:T(8,128)(2,1)S(1)}, bf16[2,2,64,344]{3,2,1,0:T(8,128)(2,1)S(1)}, u32[]{:S(2)}, u32[]{:S(2)}) collective-permute-start(bf16[2,2,64,344]{3,2,1,0:T(8,128)(2,1)S(1)} %collective-permute-done.13), channel_id=1, source_target_pairs={{0,112},{16,32},{32,16},{48,64},{64,48},{80,96},{96,80},{112,0},{1... | collective-permute-start | bytes 528392 | tf_op jit(solution)/shard_map/ppermute | solution.py:68
  170.0 16.3 %collective-permute-done.14 = bf16[2,2,64,344]{3,2,1,0:T(8,128)(2,1)S(1)} collective-permute-done((bf16[2,2,64,344]{3,2,1,0:T(8,128)(2,1)S(1)}, bf16[2,2,64,344]{3,2,1,0:T(8,128)(2,1)S(1)}, u32[]{:S(2)}, u32[]{:S(2)}) %collective-permute-start.14) | collective-permute-done | bytes 176160 | tf_op jit(solution)/shard_map/ppermute | solution.py:68
  186.3 1.1 fusion.30
  187.4 2.0 copy.148
  189.6 1.8 fusion.15
  192.2 1.3 collective-permute-done.21
  193.6 1.7 add_convert_fusion.1
  196.6 7.2 %all-to-all-start.5 = ((bf16[16,64,344]{2,1,0:T(8,128)(2,1)}), bf16[16,64,344]{2,1,0:T(8,128)(2,1)S(1)}, u32[]{:S(2)}, u32[]{:S(2)}) async-start(bf16[16,64,344]{2,1,0:T(8,128)(2,1)} %bitcast.53), calls=%async_computation.5 | async-start | bytes 1572864 | tf_op jit(solution)/shard_map/all_to_all | solution.py:51
  203.9 1.6 collective-permute-start.22
  205.4 10.9 %collective-permute-done.22 = bf16[2,172,86]{2,1,0:T(8,128)(2,1)S(1)} collective-permute-done((bf16[2,172,86]{2,1,0:T(8,128)(2,1)S(1)}, bf16[2,172,86]{2,1,0:T(8,128)(2,1)S(1)}, u32[]{:S(2)}, u32[]{:S(2)}) %collective-permute-start.22) | collective-permute-done | bytes 59200 | tf_op jit(solution)/shard_map/ppermute | solution.py:17
  217.3 1.7 convert_reduce_fusion.1
  (132 shorter events, 30.1 us)
Async XLA Ops:
  0.6 53.4 %copy-start = (bf16[2048,128]{1,0:T(8,128)(2,1)S(1)}, bf16[2048,128]{1,0:T(8,128)(2,1)}, u32[]{:S(2)}) copy-start(bf16[2048,128]{1,0:T(8,128)(2,1)} %param.8) | copy-start | bytes 1572868
  0.6 19.5 %copy-start.5 = (bf16[24,2048]{1,0:T(8,128)(2,1)S(1)}, bf16[24,2048]{1,0:T(8,128)(2,1)}, u32[]{:S(2)}) copy-start(bf16[24,2048]{1,0:T(8,128)(2,1)} %param.6) | copy-start | bytes 294916
  1.8 10.7 %collective-permute-start.15 = (bf16[2,86,128]{2,1,0:T(8,128)(2,1)S(1)}, bf16[2,86,128]{2,1,0:T(8,128)(2,1)S(1)}, u32[]{:S(2)}, u32[]{:S(2)}) collective-permute-start(bf16[2,86,128]{2,1,0:T(8,128)(2,1)S(1)} %bitcast.227), channel_id=1, source_target_pairs={{0,0},{1,32},{2,64},{3,96},{4,128},{5,160},{6,192},{7,224},{8,8},{... | collective-permute-start | bytes 132104 | tf_op jit(solution)/shard_map/ppermute | solution.py:144
  12.4 4.0 %collective-permute-start.16 = (bf16[1,2,86,128]{3,2,1,0:T(8,128)(2,1)S(1)}, bf16[1,2,86,128]{3,2,1,0:T(8,128)(2,1)S(1)}, u32[]{:S(2)}, u32[]{:S(2)}) collective-permute-start(bf16[1,2,86,128]{3,2,1,0:T(8,128)(2,1)S(1)} %bitcast.228), channel_id=1, source_target_pairs={{0,128},{128,0},{1,129},{129,1},{2,130},{130,2},{3,131},{131,3},{4... | collective-permute-start | bytes 132104 | tf_op jit(solution)/shard_map/ppermute | solution.py:17
  16.5 7.1 %collective-permute-start.17 = (bf16[2,2,86,128]{3,2,1,0:T(8,128)(2,1)S(1)}, bf16[2,2,86,128]{3,2,1,0:T(8,128)(2,1)S(1)}, u32[]{:S(2)}, u32[]{:S(2)}) collective-permute-start(bf16[2,2,86,128]{3,2,1,0:T(8,128)(2,1)S(1)} %maximum_select_fusion.13), channel_id=1, source_target_pairs={{0,1},{1,0},{2,3},{3,2},{4,5},{5,4},{6,7},{7,6},{8,9},{9,8},{10,11... | collective-permute-start | bytes 264200 | tf_op jit(solution)/shard_map/ppermute | solution.py:17
  20.1 6.9 %collective-permute-start = (bf16[1,36,2048]{2,1,0:T(8,128)(2,1)S(1)}, bf16[1,36,2048]{2,1,0:T(8,128)(2,1)S(1)}, u32[]{:S(2)}, u32[]{:S(2)}) collective-permute-start(bf16[1,36,2048]{2,1,0:T(8,128)(2,1)S(1)} %maximum_bitcast_fusion), channel_id=1, source_target_pairs={{0,1},{1,0},{2,3},{3,2},{4,5},{5,4},{6,7},{7,6},{8,9},{9,8},{10,11... | collective-permute-start | bytes 442376 | tf_op jit(solution)/shard_map/ppermute | solution.py:17
  23.6 10.0 %collective-permute-start.18 = (bf16[2,2,86,256]{3,2,1,0:T(8,128)(2,1)S(1)}, bf16[2,2,86,256]{3,2,1,0:T(8,128)(2,1)S(1)}, u32[]{:S(2)}, u32[]{:S(2)}) collective-permute-start(bf16[2,2,86,256]{3,2,1,0:T(8,128)(2,1)S(1)} %maximum_select_fusion.7), channel_id=1, source_target_pairs={{0,2},{2,0},{4,6},{6,4},{1,3},{3,1},{5,7},{7,5},{8,10},{10,8},{12,... | collective-permute-start | bytes 528392 | tf_op jit(solution)/shard_map/ppermute | solution.py:147
  27.3 19.4 %collective-permute-start.1 = (bf16[2,36,2048]{2,1,0:T(8,128)(2,1)S(1)}, bf16[2,36,2048]{2,1,0:T(8,128)(2,1)S(1)}, u32[]{:S(2)}, u32[]{:S(2)}) collective-permute-start(bf16[2,36,2048]{2,1,0:T(8,128)(2,1)S(1)} %get-tuple-element.7), channel_id=1, source_target_pairs={{0,2},{2,4},{4,6},{6,0},{1,3},{3,5},{5,7},{7,1},{8,10},{10,12},{12... | collective-permute-start | bytes 884744 | tf_op jit(solution)/shard_map/ppermute | solution.py:17
  31.8 17.1 %collective-permute-start.2 = (bf16[2,36,2048]{2,1,0:T(8,128)(2,1)S(1)}, bf16[2,36,2048]{2,1,0:T(8,128)(2,1)S(1)}, u32[]{:S(2)}, u32[]{:S(2)}) collective-permute-start(bf16[2,36,2048]{2,1,0:T(8,128)(2,1)S(1)} %get-tuple-element.7), channel_id=1, source_target_pairs={{0,6},{2,0},{4,2},{6,4},{1,7},{3,1},{5,3},{7,5},{8,14},{10,8},{12,... | collective-permute-start | bytes 884744 | tf_op jit(solution)/shard_map/ppermute | solution.py:17
  31.9 17.1 %collective-permute-start.3 = (bf16[2,36,2048]{2,1,0:T(8,128)(2,1)S(1)}, bf16[2,36,2048]{2,1,0:T(8,128)(2,1)S(1)}, u32[]{:S(2)}, u32[]{:S(2)}) collective-permute-start(bf16[2,36,2048]{2,1,0:T(8,128)(2,1)S(1)} %get-tuple-element.7), channel_id=1, source_target_pairs={{0,4},{2,6},{4,0},{6,2},{1,5},{3,7},{5,1},{7,3},{8,12},{10,14},{12... | collective-permute-start | bytes 884744 | tf_op jit(solution)/shard_map/ppermute | solution.py:17
  34.4 51.3 %collective-permute-start.19 = (bf16[2,2,86,512]{3,2,1,0:T(8,128)(2,1)}, bf16[2,2,86,512]{3,2,1,0:T(8,128)(2,1)}, u32[]{:S(2)}, u32[]{:S(2)}) collective-permute-start(bf16[2,2,86,512]{3,2,1,0:T(8,128)(2,1)} %maximum_select_fusion.2), channel_id=1, source_target_pairs={{2,4},{4,2},{6,0},{0,6},{3,5},{5,3},{7,1},{1,7},{10,12},{12,10},{1... | collective-permute-start | bytes 1056776 | tf_op jit(solution)/shard_map/ppermute | solution.py:148
  53.6 1.0 copy-start.3
  54.0 5.6 %collective-permute-start.7 = (bf16[2,172,64]{1,2,0:T(8,128)(2,1)S(1)}, bf16[2,172,64]{1,2,0:T(8,128)(2,1)S(1)}, u32[]{:S(2)}, u32[]{:S(2)}) collective-permute-start(bf16[2,172,64]{1,2,0:T(8,128)(2,1)S(1)} %get-tuple-element.25), channel_id=1, source_target_pairs={{0,8},{8,0},{1,9},{9,1},{2,10},{10,2},{3,11},{11,3},{4,12},{12,4},... | collective-permute-start | bytes 132104 | tf_op jit(solution)/shard_map/ppermute | solution.py:17
  55.8 16.8 %all-to-all-start = ((bf16[16,192,128]{2,1,0:T(8,128)(2,1)}), bf16[16,192,128]{2,1,0:T(8,128)(2,1)S(1)}, u32[]{:S(2)}, u32[]{:S(2)}) async-start(bf16[16,192,128]{2,1,0:T(8,128)(2,1)} %broadcast_in_dim.43), calls=%async_computation | async-start | bytes 1572864 | tf_op jit(solution)/shard_map/all_to_all | solution.py:51
  59.7 12.1 %collective-permute-start.8 = (bf16[2,172,64]{1,2,0:T(8,128)(2,1)S(1)}, bf16[2,172,64]{1,2,0:T(8,128)(2,1)S(1)}, u32[]{:S(2)}, u32[]{:S(2)}) collective-permute-start(bf16[2,172,64]{1,2,0:T(8,128)(2,1)S(1)} %get-tuple-element.35), channel_id=1, source_target_pairs={{0,128},{128,0},{1,129},{129,1},{2,130},{130,2},{3,131},{131,3},{4... | collective-permute-start | bytes 132104 | tf_op jit(solution)/shard_map/ppermute | solution.py:17
  73.5 30.0 %all-to-all-start.1 = ((bf16[8,344,128]{2,1,0:T(8,128)(2,1)}), bf16[8,344,128]{2,1,0:T(8,128)(2,1)}, u32[]{:S(2)}, u32[]{:S(2)}) async-start(bf16[8,344,128]{2,1,0:T(8,128)(2,1)} %broadcast_in_dim.90), calls=%async_computation.1 | async-start | bytes 1409024 | tf_op jit(solution)/shard_map/all_to_all | solution.py:51
  83.3 1.5 collective-permute-start.4
  84.9 6.9 %collective-permute-start.5 = (bf16[2,192,172]{1,2,0:T(8,128)(2,1)S(1)}, bf16[2,192,172]{1,2,0:T(8,128)(2,1)S(1)}, u32[]{:S(2)}, u32[]{:S(2)}) collective-permute-start(bf16[2,192,172]{1,2,0:T(8,128)(2,1)S(1)} %get-tuple-element.17), channel_id=1, source_target_pairs={{0,128},{128,0},{1,129},{129,1},{2,130},{130,2},{3,131},{131,3},{4... | collective-permute-start | bytes 396296 | tf_op jit(solution)/shard_map/ppermute | solution.py:17
  88.5 16.6 %collective-permute-start.6 = (bf16[384,1024]{1,0:T(8,128)(2,1)}, bf16[384,1024]{1,0:T(8,128)(2,1)}, u32[]{:S(2)}, u32[]{:S(2)}) collective-permute-start(bf16[384,1024]{1,0:T(8,128)(2,1)} %bitcast.187), channel_id=1, source_target_pairs={{0,8},{8,0},{1,9},{9,1},{2,10},{10,2},{3,11},{11,3},{4,12},{12,4},... | collective-permute-start | bytes 2359304 | tf_op jit(solution)/shard_map/ppermute | solution.py:17
  89.9 31.8 %collective-permute-start.20 = (bf16[4,86,1024]{2,0,1:T(4,128)(2,1)}, bf16[4,86,1024]{2,0,1:T(4,128)(2,1)}, u32[]{:S(2)}, u32[]{:S(2)}) collective-permute-start(bf16[4,86,1024]{2,0,1:T(4,128)(2,1)} %maximum_select_fusion), channel_id=1, source_target_pairs={{0,8},{8,0},{1,9},{9,1},{2,10},{10,2},{3,11},{11,3},{4,12},{12,4},... | collective-permute-start | bytes 2113544 | tf_op jit(solution)/shard_map/ppermute | solution.py:17
  104.8 1.4 copy-start.2
  111.8 26.1 %all-to-all-start.4 = ((bf16[8,2,64,344]{3,2,1,0:T(8,128)(2,1)}), bf16[8,2,64,344]{3,2,1,0:T(8,128)(2,1)}, u32[]{:S(2)}, u32[]{:S(2)}) async-start(bf16[8,2,64,344]{3,2,1,0:T(8,128)(2,1)} %copy.125), calls=%async_computation.4 | async-start | bytes 1572864 | tf_op jit(solution)/shard_map/all_to_all | solution.py:51
  118.8 5.4 %collective-permute-start.9 = (bf16[8,384,128]{2,1,0:T(8,128)(2,1)}, bf16[8,384,128]{2,1,0:T(8,128)(2,1)}, u32[]{:S(2)}, u32[]{:S(2)}) collective-permute-start(bf16[8,384,128]{2,1,0:T(8,128)(2,1)} %convolution_convert_fusion.1), channel_id=1, source_target_pairs={{0,8},{8,0},{1,9},{9,1},{2,10},{10,2},{3,11},{11,3},{4,12},{12,4},... | collective-permute-start | bytes 2359304 | tf_op jit(solution)/shard_map/ppermute | solution.py:17
  121.7 2.6 %copy-start.4 = (bf16[384,344]{0,1:T(8,128)(2,1)S(1)}, bf16[384,344]{0,1:T(8,128)(2,1)}, u32[]{:S(2)}) copy-start(bf16[384,344]{0,1:T(8,128)(2,1)} %get-tuple-element.14) | copy-start | bytes 792580
  137.8 21.8 %all-to-all-start.2 = ((bf16[16,192,128]{2,1,0:T(8,128)(2,1)}), bf16[16,192,128]{2,1,0:T(8,128)(2,1)}, u32[]{:S(2)}, u32[]{:S(2)}) async-start(bf16[16,192,128]{2,1,0:T(8,128)(2,1)} %bitcast.33), calls=%async_computation.2 | async-start | bytes 1572864 | tf_op jit(solution)/shard_map/all_to_all | solution.py:51
  146.6 4.9 %collective-permute-start.11 = (bf16[2,64,344]{2,1,0:T(8,128)(2,1)S(1)}, bf16[2,64,344]{2,1,0:T(8,128)(2,1)S(1)}, u32[]{:S(2)}, u32[]{:S(2)}) collective-permute-start(bf16[2,64,344]{2,1,0:T(8,128)(2,1)S(1)} %reduce_sum.44), channel_id=1, source_target_pairs={{0,16},{16,0},{32,48},{48,32},{64,80},{80,64},{96,112},{112,96},{1... | collective-permute-start | bytes 264200 | tf_op jit(solution)/shard_map/ppermute | solution.py:63
  149.1 44.5 %collective-permute-start.10 = (bf16[8,128,344]{1,2,0:T(8,128)(2,1)}, bf16[8,128,344]{1,2,0:T(8,128)(2,1)}, u32[]{:S(2)}, u32[]{:S(2)}) collective-permute-start(bf16[8,128,344]{1,2,0:T(8,128)(2,1)} %fusion), channel_id=1, source_target_pairs={{0,8},{8,0},{1,9},{9,1},{2,10},{10,2},{3,11},{11,3},{4,12},{12,4},... | collective-permute-start | bytes 2113544 | tf_op jit(solution)/shard_map/ppermute | solution.py:17
  151.6 7.1 %collective-permute-start.12 = (bf16[2,2,64,344]{3,2,1,0:T(8,128)(2,1)S(1)}, bf16[2,2,64,344]{3,2,1,0:T(8,128)(2,1)}, u32[]{:S(2)}, u32[]{:S(2)}) collective-permute-start(bf16[2,2,64,344]{3,2,1,0:T(8,128)(2,1)S(1)} %maximum_select_fusion.6), channel_id=1, source_target_pairs={{0,112},{16,32},{32,16},{48,64},{64,48},{80,96},{96,80},{112,0},{1... | collective-permute-start | bytes 528392 | tf_op jit(solution)/shard_map/ppermute | solution.py:68
  158.6 8.3 %collective-permute-start.13 = (bf16[2,2,64,344]{3,2,1,0:T(8,128)(2,1)}, bf16[2,2,64,344]{3,2,1,0:T(8,128)(2,1)S(1)}, u32[]{:S(2)}, u32[]{:S(2)}) collective-permute-start(bf16[2,2,64,344]{3,2,1,0:T(8,128)(2,1)} %collective-permute-done.12), channel_id=1, source_target_pairs={{0,16},{16,0},{32,48},{48,32},{64,80},{80,64},{96,112},{112,96},{1... | collective-permute-start | bytes 528392 | tf_op jit(solution)/shard_map/ppermute | solution.py:68
  162.2 34.5 %all-to-all-start.3 = ((bf16[32,64,128]{2,1,0:T(8,128)(2,1)}), bf16[32,64,128]{2,1,0:T(8,128)(2,1)}, u32[]{:S(2)}, u32[]{:S(2)}) async-start(bf16[32,64,128]{2,1,0:T(8,128)(2,1)} %bitcast.200), calls=%async_computation.3 | async-start | bytes 1048576 | tf_op jit(solution)/shard_map/all_to_all | solution.py:51
  166.9 19.4 %collective-permute-start.14 = (bf16[2,2,64,344]{3,2,1,0:T(8,128)(2,1)S(1)}, bf16[2,2,64,344]{3,2,1,0:T(8,128)(2,1)S(1)}, u32[]{:S(2)}, u32[]{:S(2)}) collective-permute-start(bf16[2,2,64,344]{3,2,1,0:T(8,128)(2,1)S(1)} %collective-permute-done.13), channel_id=1, source_target_pairs={{0,112},{16,32},{32,16},{48,64},{64,48},{80,96},{96,80},{112,0},{1... | collective-permute-start | bytes 528392 | tf_op jit(solution)/shard_map/ppermute | solution.py:68
  189.4 2.0 copy-start.1
  192.1 1.4 collective-permute-start.21
  196.6 22.4 %all-to-all-start.5 = ((bf16[16,64,344]{2,1,0:T(8,128)(2,1)}), bf16[16,64,344]{2,1,0:T(8,128)(2,1)S(1)}, u32[]{:S(2)}, u32[]{:S(2)}) async-start(bf16[16,64,344]{2,1,0:T(8,128)(2,1)} %bitcast.53), calls=%async_computation.5 | async-start | bytes 1572864 | tf_op jit(solution)/shard_map/all_to_all | solution.py:51
  203.9 12.5 %collective-permute-start.22 = (bf16[2,172,86]{2,1,0:T(8,128)(2,1)S(1)}, bf16[2,172,86]{2,1,0:T(8,128)(2,1)S(1)}, u32[]{:S(2)}, u32[]{:S(2)}) collective-permute-start(bf16[2,172,86]{2,1,0:T(8,128)(2,1)S(1)} %fusion.26), channel_id=1, source_target_pairs={{0,128},{128,0},{1,129},{129,1},{2,130},{130,2},{3,131},{131,3},{4... | collective-permute-start | bytes 177512 | tf_op jit(solution)/shard_map/ppermute | solution.py:17
